TPU v7x, 256 devices: a whole 4x4x8 slice. The times are simulated.
256 devices in a mesh: space: 32 (over y, x, core), chan: 8 (over z).
Axes of the slice: x: 4, y: 4, z: 8, core: 2. Of those that a mesh axis runs over, the one named last changes fastest.
Arguments:
- members: bfloat16 [8, 96, 8, 17280], P(None, 'space', 'chan'), may hold values from -400 to 400, as said below
- gain: float32 [768], P('chan'), may hold values from 0.5 to 1.5
- shift: float32 [768], P('chan'), may hold values from -3 to 3
- w_first: bfloat16 [2, 8, 96, 96], P(None, 'chan'), may hold values from -0.4375 to 0.4375
- b_first: float32 [2, 8, 96], P(None, 'chan'), may hold values from -3 to 3
- w_second: bfloat16 [2, 8, 96, 96], P(None, 'chan'), may hold values from -0.4375 to 0.4375
- b_second: float32 [2, 8, 96], P(None, 'chan'), may hold values from -3 to 3
- cotangent: bfloat16 [8, 96, 8, 17280], P(None, 'space', 'chan'), may hold values from -6 to 6
Outputs:
- mixed: bfloat16 [8, 96, 8, 17280], P(None, 'space', 'chan')
- grad_input: bfloat16 [8, 96, 8, 17280], P(None, 'space', 'chan')
- grad_w_first: float32 [2, 8, 96, 96], P(None, 'chan')
- grad_b_first: float32 [2, 8, 96], P(None, 'chan')
- grad_w_second: float32 [2, 8, 96, 96], P(None, 'chan')
- grad_b_second: float32 [2, 8, 96], P(None, 'chan')
- grad_gain: float32 [768], P('chan')
- grad_shift: float32 [768], P('chan')
Inputs may be any that keep to these rules, and one draw needn't show every extreme that they name: `members`: real values of varying channel scale.
All inputs are finite; a program needn't handle non-finite values.
Results may differ from a plain program's by a relative error of at most 0.019.
The roundings to bfloat16 on the way count: a program that leaves them out, or rounds other values in their place, can miss the bound.
Values may be sent and summed in bfloat16 or wider, within the bound.
A program may use at most 64 MiB of HBM per device.

v0:
```python
import math

import jax
import jax.numpy as jnp
import ml_dtypes
import numpy as np
from jax import lax
from jax.experimental import pallas as pl
from jax.experimental.pallas import tpu as pltpu
from jax.sharding import PartitionSpec as P

C = 768
CB = 96
W = 180
WP = 192
MW = 64
H = 96
NS = 32
NC = 8
HL = H // NS
LN = 128
QL = 4 * LN

shrink_level = 0.05
norm_epsilon = 1e-05
gelu_scale = 0.7978845608
gelu_cubic = 0.044715
lon_factor = 1.0 / math.sqrt(W)
lat_factor = 1.0 / math.sqrt(H)

F32 = jnp.float32
BF16 = jnp.bfloat16
MESH = pl.DeviceIdType.MESH

RS1, AG1, A2, A1, A4, A3, GWR, GWG, RS2, AG2, GG = range(11)


def twiddle(length, columns):
    rows = np.arange(length)[:, None]
    cols = np.arange(columns)[None, :]
    angles = (rows * cols % length).astype(np.float32) * np.float32(2.0 * math.pi / length)
    return (
        np.cos(angles).astype(np.float32),
        np.sin(angles).astype(np.float32),
    )


def tables():
    bf = ml_dtypes.bfloat16
    cos_lon, sin_lon = (t.astype(bf).astype(np.float32) for t in twiddle(W, MW))
    cos_lat, sin_lat = (t.astype(bf).astype(np.float32) for t in twiddle(H, H))
    lon = np.zeros((NS, 2, 2, 2, 2, WP), np.float32)
    scaled = np.zeros_like(lon)
    for d in range(NS):
        for mm in range(2):
            m = 2 * d + mm
            twice = 1.0 if m == 0 else 2.0
            for b in range(2):
                lon[d, 0, mm, b, b, :W] = cos_lon[:, m]
                lon[d, 1, mm, b, b, :W] = -sin_lon[:, m]
                scaled[d, :, mm, b] = twice * lon[d, :, mm, b]
    lon = lon.reshape(8 * NS, 2 * WP)
    scaled = scaled.reshape(8 * NS, 2 * WP)
    lat = np.zeros((HL, 2, 2, 2, H, NS, 2, 2, 2), np.float32)
    for hh in range(HL):
        cos_part = cos_lat[:, hh::HL]
        sin_part = sin_lat[:, hh::HL]
        for mm in range(2):
            for b in range(2):
                lat[hh, mm, b, 0, :, :, 0, mm, b] = cos_part
                lat[hh, mm, b, 0, :, :, 1, mm, b] = sin_part
                lat[hh, mm, b, 1, :, :, 0, mm, b] = -sin_part
                lat[hh, mm, b, 1, :, :, 1, mm, b] = cos_part
    lat = lat.reshape(HL, 8 * H, 8 * NS)
    return (
        np.stack([lon, scaled]).astype(bf),
        np.stack([lon.T, scaled.T]).astype(bf),
        lat.astype(bf),
        np.swapaxes(lat, 1, 2).astype(bf),
    )


def dot(left, right):
    return lax.dot_general(left, right, (((1,), (0,)), ((), ())), preferred_element_type=F32)


def dot_nt(left, right):
    return lax.dot_general(left, right, (((1,), (1,)), ((), ())), preferred_element_type=F32)


def dot_tn(left, right):
    return lax.dot_general(left, right, (((0,), (0,)), ((), ())), preferred_element_type=F32)


def unpack(source, target, h):
    lane = lax.broadcasted_iota(jnp.int32, (8, LN), 1)

    def step(it, carry):
        for u in range(15):
            i = it * 15 + u
            chunk = source[h, 0, :, pl.ds(pl.multiple_of(i * 384, 128), 384)].astype(F32)
            v0, v1, v2 = chunk[:, :128], chunk[:, 128:256], chunk[:, 256:]
            parts = (
                v0,
                pltpu.roll(jnp.where(lane >= 96, v0, v1), 32, 1),
                pltpu.roll(jnp.where(lane >= 64, v1, v2), 64, 1),
                pltpu.roll(v2, 96, 1),
            )
            for q in range(4):
                target[h, pl.ds(pl.multiple_of(i * 32 + 8 * q, 8), 8), :] = jnp.where(
                    lane < CB, parts[q], 0.0
                )
        return carry

    lax.fori_loop(0, 3, step, 0)


def pack(source, target, h):
    lane = lax.broadcasted_iota(jnp.int32, (8, LN), 1)

    def step(it, carry):
        for u in range(15):
            i = it * 15 + u
            p0, p1, p2, p3 = (
                source[h, pl.ds(pl.multiple_of(i * 32 + 8 * q, 8), 8), :] for q in range(4)
            )
            r1 = pltpu.roll(p1, 96, 1)
            r2 = pltpu.roll(p2, 64, 1)
            r3 = pltpu.roll(p3, 32, 1)
            chunk = jnp.concatenate(
                [
                    jnp.where(lane < 96, p0, r1),
                    jnp.where(lane < 64, r1, r2),
                    jnp.where(lane < 32, r2, r3),
                ],
                axis=1,
            )
            target[h, 0, :, pl.ds(pl.multiple_of(i * 384, 128), 384)] = chunk.astype(BF16)
        return carry

    lax.fori_loop(0, 3, step, 0)


def layer(
    x_hbm, cot_hbm, gain_ref, shift_ref, w1_ref, b1_ref, w2_ref, b2_ref,
    d_hbm, e_hbm, l_hbm, m_hbm,
    mixed_hbm, gin_hbm, gw1_ref, gb1_ref, gw2_ref, gb2_ref, gg_ref, gs_ref,
    xv, cv, dv, ev, lv, mv, tx, tc, xn, cen, gc,
    send1, send2, send3, send4, recv1, recv2, recv3, recv4, rc,
    lt, gsh, hid, gpost, gpre, sh, glat, wc, vec,
    acc, st, rb, ags, ab, at, st2, rb2, ags2, ab2, at2,
    gb, gr, gas, ga, ggs, ggr,
    in_sems, out_sems, send_sems, recv_sems,
):
    me_s = lax.axis_index("space")
    me_c = lax.axis_index("chan")

    loads = [pltpu.make_async_copy(x_hbm.at[h], xv.at[h], in_sems.at[h]) for h in range(HL)]
    loads += [pltpu.make_async_copy(cot_hbm.at[h], cv.at[h], in_sems.at[3 + h]) for h in range(HL)]
    loads += [
        pltpu.make_async_copy(d_hbm, dv, in_sems.at[6]),
        pltpu.make_async_copy(e_hbm, ev, in_sems.at[7]),
        pltpu.make_async_copy(l_hbm, lv, in_sems.at[8]),
        pltpu.make_async_copy(m_hbm, mv, in_sems.at[9]),
    ]
    for load in loads:
        load.start()

    barrier = pltpu.get_barrier_semaphore()

    def greet_space(r, carry):
        pl.semaphore_signal(
            barrier, inc=1, device_id={"space": lax.rem(me_s + r, NS)}, device_id_type=MESH
        )
        return carry

    def greet_chan(r, carry):
        pl.semaphore_signal(
            barrier, inc=1, device_id={"chan": lax.rem(me_c + r, NC)}, device_id_type=MESH
        )
        return carry

    lax.fori_loop(1, NC, greet_chan, 0)
    lax.fori_loop(1, NS, greet_space, 0)

    def spread(axis, index, piece, target):
        count, me = (NS, me_s) if axis == "space" else (NC, me_c)

        def step(r, carry):
            t = lax.rem(me + r, count)
            pltpu.make_async_remote_copy(
                src_ref=piece(t),
                dst_ref=target.at[me],
                send_sem=send_sems.at[index],
                recv_sem=recv_sems.at[index],
                device_id={axis: t},
                device_id_type=MESH,
            ).start()
            return carry

        lax.fori_loop(1, count, step, 0)
        pltpu.make_async_copy(piece(me), target.at[me], recv_sems.at[index]).start()

    def arrived(index, target):
        pltpu.make_async_copy(target, target, recv_sems.at[index]).wait()

    def sent(index, target, count):
        rest = target.at[pl.ds(0, count - 1)]
        pltpu.make_async_copy(rest, rest, send_sems.at[index]).wait()

    vec[...] = jnp.zeros_like(vec)
    vec[0:1, 0:CB] = gain_ref[...]
    vec[1:2, 0:CB] = shift_ref[...]
    for layer_at, (b_ref, w_ref) in enumerate(((b1_ref, w1_ref), (b2_ref, w2_ref))):
        vec[2 + layer_at : 3 + layer_at, 0:CB] = b_ref[0]
        vec[2 + layer_at : 3 + layer_at, LN : LN + CB] = b_ref[1]
        wc[layer_at] = jnp.zeros((2 * LN, 2 * LN), BF16)
        w_real, w_imag = w_ref[0, 0], w_ref[1, 0]
        wc[layer_at, 0:CB, 0:CB] = w_real
        wc[layer_at, 0:CB, LN : LN + CB] = w_imag
        wc[layer_at, LN : LN + CB, 0:CB] = -w_imag
        wc[layer_at, LN : LN + CB, LN : LN + CB] = w_real
    tx[:, 8 * W :, :] = jnp.zeros((HL, 8 * (WP - W), LN), F32)
    tc[:, 8 * W :, :] = jnp.zeros((HL, 8 * (WP - W), LN), F32)
    acc[...] = jnp.zeros_like(acc)
    ab[NC:] = jnp.zeros((NC, 8, 256), F32)
    ab2[NC:] = jnp.zeros((NC, 8, 256), F32)

    lane_w = lax.broadcasted_iota(jnp.int32, (WP, LN), 1)

    def members_of(array, h, b):
        return array[h, pl.ds(b, WP, stride=8), :]

    def pieces_of_sums(target):
        for hi in range(2):
            turned = jnp.transpose(acc[hi])
            for lo in range(4):
                target[4 * hi + lo] = turned[8 * lo : 8 * lo + 8, :]

    for h in range(HL):
        loads[h].wait()
        unpack(xv, tx, h)
    for hi in range(2):
        total = jnp.zeros((WP, LN), F32)
        for lo in range(4):
            for h in range(HL):
                tile = members_of(tx, h, 4 * hi + lo)
                one = jnp.sum(tile, axis=1, keepdims=True)
                two = jnp.sum(tile * tile, axis=1, keepdims=True)
                total = jnp.where(lane_w == 8 * lo + h, one, total)
                total = jnp.where(lane_w == 8 * lo + 3 + h, two, total)
        acc[hi, 0:WP, :] = total
    pieces_of_sums(st)
    pl.semaphore_wait(barrier, NS - 1 + NC - 1)
    spread("chan", RS1, lambda t: st.at[t], rb)

    for h in range(HL):
        loads[3 + h].wait()
        unpack(cv, tc, h)
    loads[6].wait()
    for h in range(HL):
        for b in range(8):
            hi, lo = divmod(b, 4)
            xn[h, WP * hi : WP * hi + WP, LN * lo : LN * lo + LN] = members_of(tc, h, b).astype(
                BF16
            )
        out = dot(dv[1], xn[h]) * lon_factor
        send2[:, :, QL * h : QL * h + QL] = out.reshape(NS, 8, QL).astype(BF16)

    arrived(RS1, rb)
    sums = jnp.sum(rb[...], axis=0) * (1.0 / C)
    mean = sums
    var_in = pltpu.roll(sums, 5, 0)
    inv = lax.rsqrt(var_in - mean * mean + norm_epsilon)
    row8 = lax.broadcasted_iota(jnp.int32, (8, 256), 0)
    ags[...] = jnp.where(row8 < 3, mean, jnp.where(row8 < 6, pltpu.roll(inv, 3, 0), 0.0))
    spread("chan", AG1, lambda t: ags, ab)
    spread("space", A2, lambda t: send2.at[t], recv2)

    arrived(AG1, ab.at[pl.ds(0, NC)])
    at[...] = jnp.transpose(ab[...].reshape(2 * NC * 8, 256))
    gain_row = vec[0:1, 0:LN]
    shift_row = vec[1:2, 0:LN]
    for h in range(HL):
        for b in range(8):
            hi, lo = divmod(b, 4)
            mean_col = at[0:WP, 8 * b + h : 8 * b + h + 1]
            inv_col = at[0:WP, 8 * b + 3 + h : 8 * b + 4 + h]
            centred = (members_of(tx, h, b) - mean_col) * inv_col
            rows, lanes = pl.ds(WP * hi, WP), pl.ds(LN * lo, LN)
            cen[h, rows, lanes] = centred
            xn[h, rows, lanes] = (centred * gain_row + shift_row).astype(BF16)
        out = dot(dv[0], xn[h]) * lon_factor
        send1[:, :, QL * h : QL * h + QL] = out.reshape(NS, 8, QL).astype(BF16)
    spread("space", A1, lambda t: send1.at[t], recv1)

    def latitude(received, target, ones):
        lane = lax.broadcasted_iota(jnp.int32, (H, LN), 1)
        for h in range(HL):
            rc[h] = received[:, :, QL * h : QL * h + QL].reshape(8 * NS, QL)

        def step(g, carry):
            rows = pl.ds(pl.multiple_of(g * 192, 192), 192)
            out = dot(lv[0, rows, :], rc[0])
            for h in range(1, HL):
                out = out + dot(lv[h, rows, :], rc[h])
            out = out * lat_factor
            for part in range(2):
                for lo in range(4):
                    tile = out[H * part : H * part + H, LN * lo : LN * lo + LN]
                    if ones and part == 0:
                        tile = jnp.where(lane == CB, 1.0, tile)
                    target[g, H * lo : H * lo + H, LN * part : LN * part + LN] = tile.astype(BF16)
            return carry

        lax.fori_loop(0, 4, step, 0)

    loads[8].wait()
    arrived(A2, recv2)
    latitude(recv2, gsh, False)
    arrived(A1, recv1)
    latitude(recv1, lt, True)

    def mix(g, carry):
        lane = lax.broadcasted_iota(jnp.int32, (4 * H, 2 * LN), 1)
        pre = dot(lt[g], wc[0]) + vec[2:3, :]
        t = jnp.tanh(gelu_scale * (pre + gelu_cubic * pre * pre * pre))
        hidden = 0.5 * pre * (1.0 + t)
        hidden = jnp.where(lane == CB, 1.0, hidden).astype(BF16)
        slope = 0.5 * (1.0 + t) + 0.5 * pre * (1.0 - t * t) * gelu_scale * (
            1.0 + 3.0 * gelu_cubic * pre * pre
        )
        hid[g] = hidden
        post = dot(hidden, wc[1]) + vec[3:4, :]
        s = jnp.tanh(post * (1.0 / shrink_level))
        shrunk = (post - shrink_level * s).astype(BF16)
        grad_post = (gsh[g].astype(F32) * (s * s)).astype(BF16)
        gpost[g] = grad_post
        grad_pre = (dot_nt(grad_post, wc[1]) * slope).astype(BF16)
        gpre[g] = grad_pre
        grad_lat = dot_nt(grad_pre, wc[0]).astype(BF16)
        for part in range(2):
            for lo in range(4):
                rows, lanes = slice(H * part, H * part + H), slice(LN * lo, LN * lo + LN)
                from_rows = slice(H * lo, H * lo + H)
                from_lanes = slice(LN * part, LN * part + LN)
                sh[g, rows, lanes] = shrunk[from_rows, from_lanes]
                glat[g, rows, lanes] = grad_lat[from_rows, from_lanes]
        return carry

    lax.fori_loop(0, 4, mix, 0)

    def back(source, target):
        spectrum = source[...].reshape(8 * H, QL)
        for h in range(HL):
            out = dot(mv[h], spectrum) * lat_factor
            target[:, :, QL * h : QL * h + QL] = out.reshape(NS, 8, QL).astype(BF16)

    loads[9].wait()
    back(glat, send4)
    spread("space", A4, lambda t: send4.at[t], recv4)
    back(sh, send3)
    spread("space", A3, lambda t: send3.at[t], recv3)

    for layer_at, (left, right) in enumerate(((lt, gpre), (hid, gpost))):
        outer = dot_tn(left[...].reshape(16 * H, 2 * LN), right[...].reshape(16 * H, 2 * LN))
        real = outer[0:LN, 0:LN] + outer[LN:, LN:]
        imag = outer[0:LN, LN:] - outer[LN:, 0:LN]
        gb[16 * layer_at : 16 * layer_at + 8] = real.reshape(8, 16, LN).astype(BF16)
        gb[16 * layer_at + 8 : 16 * layer_at + 16] = imag.reshape(8, 16, LN).astype(BF16)
    spread("space", GWR, lambda t: gb.at[t], gr)

    loads[7].wait()
    arrived(A4, recv4)
    gain_sum = jnp.zeros((8, LN), F32)
    shift_sum = jnp.zeros((8, LN), F32)
    totals = [jnp.zeros((WP, LN), F32), jnp.zeros((WP, LN), F32)]
    for h in range(HL):
        out = dot(ev[0], recv4[:, :, QL * h : QL * h + QL].reshape(8 * NS, QL)) * lon_factor
        for b in range(8):
            hi, lo = divmod(b, 4)
            rows, lanes = slice(WP * hi, WP * hi + WP), slice(LN * lo, LN * lo + LN)
            grad_normed = out[rows, lanes]
            centred = cen[h, rows, lanes]
            gain_sum = gain_sum + jnp.sum((grad_normed * centred).reshape(WP // 8, 8, LN), axis=0)
            shift_sum = shift_sum + jnp.sum(grad_normed.reshape(WP // 8, 8, LN), axis=0)
            grad_centred = grad_normed * gain_row
            gc[h, rows, lanes] = grad_centred
            one = jnp.sum(grad_centred, axis=1, keepdims=True)
            two = jnp.sum(grad_centred * centred, axis=1, keepdims=True)
            totals[hi] = jnp.where(lane_w == 8 * lo + h, one, totals[hi])
            totals[hi] = jnp.where(lane_w == 8 * lo + 3 + h, two, totals[hi])
    for hi in range(2):
        acc[hi, 0:WP, :] = totals[hi]
    pieces_of_sums(st2)
    spread("chan", RS2, lambda t: st2.at[t], rb2)
    ggs[0:1, :] = jnp.sum(gain_sum, axis=0, keepdims=True)
    ggs[1:2, :] = jnp.sum(shift_sum, axis=0, keepdims=True)
    spread("space", GG, lambda t: ggs, ggr)

    arrived(GWR, gr)
    gas[...] = jnp.sum(gr[...].astype(F32), axis=0).astype(BF16)
    spread("space", GWG, lambda t: gas, ga)

    arrived(A3, recv3)
    stores = []

    def put_mixed(h):
        out = dot(ev[1], recv3[:, :, QL * h : QL * h + QL].reshape(8 * NS, QL)) * lon_factor
        for b in range(8):
            hi, lo = divmod(b, 4)
            tc[h, pl.ds(b, WP, stride=8), :] = out[
                WP * hi : WP * hi + WP, LN * lo : LN * lo + LN
            ]
        pack(tc, cv, h)
        store = pltpu.make_async_copy(cv.at[h], mixed_hbm.at[h], out_sems.at[h])
        store.start()
        stores.append(store)

    put_mixed(0)
    arrived(RS2, rb2)
    ags2[...] = jnp.sum(rb2[...], axis=0) * (1.0 / C)
    spread("chan", AG2, lambda t: ags2, ab2)
    put_mixed(1)
    put_mixed(2)

    arrived(AG2, ab2.at[pl.ds(0, NC)])
    at2[...] = jnp.transpose(ab2[...].reshape(2 * NC * 8, 256))
    for h in range(HL):
        for b in range(8):
            hi, lo = divmod(b, 4)
            rows, lanes = slice(WP * hi, WP * hi + WP), slice(LN * lo, LN * lo + LN)
            inv_col = at[0:WP, 8 * b + 3 + h : 8 * b + 4 + h]
            first = at2[0:WP, 8 * b + h : 8 * b + h + 1]
            second = at2[0:WP, 8 * b + 3 + h : 8 * b + 4 + h]
            tx[h, pl.ds(b, WP, stride=8), :] = inv_col * (
                gc[h, rows, lanes] - first - cen[h, rows, lanes] * second
            )
        pack(tx, xv, h)
        store = pltpu.make_async_copy(xv.at[h], gin_hbm.at[h], out_sems.at[3 + h])
        store.start()
        stores.append(store)

    arrived(GG, ggr)
    both = jnp.sum(ggr[...], axis=0)
    gg_ref[...] = both[0:1, 0:CB]
    gs_ref[...] = both[1:2, 0:CB]
    arrived(GWG, ga)
    for layer_at, (gw_ref, gbias_ref) in enumerate(((gw1_ref, gb1_ref), (gw2_ref, gb2_ref))):
        for part in range(2):
            at_piece = 16 * layer_at + 8 * part
            block = ga[at_piece : at_piece + 8].astype(F32).reshape(LN, LN)
            gw_ref[part, 0] = block[0:CB, 0:CB]
            gbias_ref[part] = block[CB : CB + 1, 0:CB]

    sent(RS1, rb, NC)
    sent(AG1, ab, NC)
    sent(RS2, rb2, NC)
    sent(AG2, ab2, NC)
    sent(A2, recv2, NS)
    sent(A1, recv1, NS)
    sent(A4, recv4, NS)
    sent(A3, recv3, NS)
    sent(GWR, gr, NS)
    sent(GWG, ga, NS)
    sent(GG, ggr, NS)
    for store in stores:
        store.wait()


def on_device(members, gain, shift, w_first, b_first, w_second, b_second, cotangent):
    lon_out, lon_back, lat_out, lat_back = (jnp.asarray(t) for t in tables())
    anywhere = pl.BlockSpec(memory_space=pl.ANY)
    vmem = pl.BlockSpec(memory_space=pltpu.VMEM)
    token = (HL, 1, 8, W * CB)
    piece = (NS, 8, HL * QL)
    spectral = (4, 4 * H, 2 * LN)
    folded = (4, 2 * H, QL)
    outs = pl.pallas_call(
        layer,
        out_shape=(
            jax.ShapeDtypeStruct(token, BF16),
            jax.ShapeDtypeStruct(token, BF16),
            jax.ShapeDtypeStruct((2, 1, CB, CB), F32),
            jax.ShapeDtypeStruct((2, 1, CB), F32),
            jax.ShapeDtypeStruct((2, 1, CB, CB), F32),
            jax.ShapeDtypeStruct((2, 1, CB), F32),
            jax.ShapeDtypeStruct((1, CB), F32),
            jax.ShapeDtypeStruct((1, CB), F32),
        ),
        in_specs=[anywhere] * 2 + [vmem] * 6 + [anywhere] * 4,
        out_specs=tuple([anywhere] * 2 + [vmem] * 6),
        scratch_shapes=[
            pltpu.VMEM(token, BF16),
            pltpu.VMEM(token, BF16),
            pltpu.VMEM((2, 8 * NS, 2 * WP), BF16),
            pltpu.VMEM((2, 2 * WP, 8 * NS), BF16),
            pltpu.VMEM((HL, 8 * H, 8 * NS), BF16),
            pltpu.VMEM((HL, 8 * NS, 8 * H), BF16),
            pltpu.VMEM((HL, 8 * WP, LN), F32),
            pltpu.VMEM((HL, 8 * WP, LN), F32),
            pltpu.VMEM((HL, 2 * WP, QL), BF16),
            pltpu.VMEM((HL, 2 * WP, QL), F32),
            pltpu.VMEM((HL, 2 * WP, QL), F32),
        ]
        + [pltpu.VMEM(piece, BF16)] * 8
        + [pltpu.VMEM((HL, 8 * NS, QL), BF16)]
        + [pltpu.VMEM(spectral, BF16)] * 5
        + [pltpu.VMEM(folded, BF16)] * 2
        + [
            pltpu.VMEM((2, 2 * LN, 2 * LN), BF16),
            pltpu.VMEM((8, 2 * LN), F32),
            pltpu.VMEM((2, 256, LN), F32),
        ]
        + [
            pltpu.VMEM((NC, 8, 256), F32),
            pltpu.VMEM((NC, 8, 256), F32),
            pltpu.VMEM((8, 256), F32),
            pltpu.VMEM((2 * NC, 8, 256), F32),
            pltpu.VMEM((256, 2 * NC * 8), F32),
        ]
        * 2
        + [
            pltpu.VMEM((NS, 16, LN), BF16),
            pltpu.VMEM((NS, 16, LN), BF16),
            pltpu.VMEM((16, LN), BF16),
            pltpu.VMEM((NS, 16, LN), BF16),
            pltpu.VMEM((2, LN), F32),
            pltpu.VMEM((NS, 2, LN), F32),
            pltpu.SemaphoreType.DMA((10,)),
            pltpu.SemaphoreType.DMA((6,)),
            pltpu.SemaphoreType.DMA((11,)),
            pltpu.SemaphoreType.DMA((11,)),
        ],
        compiler_params=pltpu.CompilerParams(
            collective_id=0, has_side_effects=True, vmem_limit_bytes=56 * 1024 * 1024
        ),
    )(
        jnp.transpose(members, (1, 2, 0, 3)),
        jnp.transpose(cotangent, (1, 2, 0, 3)),
        gain.reshape(1, CB),
        shift.reshape(1, CB),
        w_first,
        b_first,
        w_second,
        b_second,
        lon_out,
        lon_back,
        lat_out,
        lat_back,
    )
    mixed, grad_input, gw1, gb1, gw2, gb2, gg, gs = outs
    return (
        jnp.transpose(mixed, (2, 0, 1, 3)),
        jnp.transpose(grad_input, (2, 0, 1, 3)),
        gw1,
        gb1,
        gw2,
        gb2,
        gg.reshape(CB),
        gs.reshape(CB),
    )


def solution(mesh):
    placed = (
        P(None, "space", "chan", None),
        P("chan"),
        P("chan"),
        P(None, "chan", None, None),
        P(None, "chan", None),
        P(None, "chan", None, None),
        P(None, "chan", None),
        P(None, "space", "chan", None),
    )
    return jax.shard_map(
        on_device,
        mesh=mesh,
        in_specs=placed,
        out_specs=(
            P(None, "space", "chan", None),
            P(None, "space", "chan", None),
            P(None, "chan", None, None),
            P(None, "chan", None),
            P(None, "chan", None, None),
            P(None, "chan", None),
            P("chan"),
            P("chan"),
        ),
        check_vma=False,
    )
```

profile of v0, /device:TPU:1, one launch (start us, length us, event | category | flops | bytes accessed | tf_op | source)
XLA Modules:
  0.0 81.4 jit_solution(15010360323556183622)
XLA Ops:
  0.6 74.2 %shard_map.179 = (bf16[3,1,8,17280]{3,2,1,0:T(8,128)(2,1)}, bf16[3,1,8,17280]{3,2,1,0:T(8,128)(2,1)}, f32[2,1,96,96]{3,2,1,0:T(8,128)}, f32[2,1,96]{2,1,0:T(1,12...) custom-call(bf16[3,1,8,17280]{3,2,1,0:T(8,128)(2,1)} %bitcast.8, ...), custom_call_target="tpu_custom_call" | custom-call | tf_op jit(solution)/shard_map/pallas_call | solution.py:479
  74.8 0.0 copy-start
  74.8 2.2 %copy.28 = bf16[8,3,1,17280]{3,0,2,1:T(8,128)(2,1)} copy(bf16[8,3,1,17280]{3,0,2,1:T(8,128)(2,1)} %bitcast.11) | data formatting | bytes 1658880
  77.0 0.0 copy-done
  77.0 0.0 copy-start.2
  77.0 0.0 copy-start.4
  77.0 0.0 copy-start.1
  77.0 0.0 copy-start.3
  77.0 0.0 copy-start.6
  77.0 0.0 copy-start.5
  77.0 0.9 %copy.29 = bf16[8,3,1,17280]{3,0,2,1:T(8,128)(2,1)} copy(bf16[8,3,1,17280]{3,0,2,1:T(8,128)(2,1)S(1)} %bitcast.10) | data formatting | bytes 1658880
  77.9 0.0 copy-done.2
  77.9 0.6 copy.30
  78.6 0.0 copy-done.4
  78.6 0.6 copy.31
  79.1 0.0 copy-done.1
  79.1 0.6 copy.32
  79.8 0.0 copy-done.3
  79.8 0.6 copy.33
  80.4 0.0 copy-done.6
  80.4 0.5 copy.34
  80.9 0.0 copy-done.5
  80.9 0.5 copy.35
Async XLA Ops:
  74.8 2.2 %copy-start = (bf16[3,1,8,17280]{3,2,1,0:T(8,128)(2,1)S(1)}, bf16[3,1,8,17280]{3,2,1,0:T(8,128)(2,1)}, u32[]{:S(2)}) copy-start(bf16[3,1,8,17280]{3,2,1,0:T(8,128)(2,1)} %get-tuple-element.17) | copy-start | bytes 2488324
  77.0 0.9 %copy-start.2 = (f32[2,1,96,96]{3,2,1,0:T(8,128)S(1)}, f32[2,1,96,96]{3,2,1,0:T(8,128)}, u32[]{:S(2)}) copy-start(f32[2,1,96,96]{3,2,1,0:T(8,128)} %get-tuple-element.34) | copy-start | bytes 221188
  77.0 1.6 %copy-start.4 = (f32[2,1,96]{2,1,0:T(1,128)S(1)}, f32[2,1,96]{2,1,0:T(1,128)}, u32[]{:S(2)}) copy-start(f32[2,1,96]{2,1,0:T(1,128)} %get-tuple-element.35) | copy-start | bytes 2308
  77.0 2.1 %copy-start.1 = (f32[2,1,96,96]{3,2,1,0:T(8,128)S(1)}, f32[2,1,96,96]{3,2,1,0:T(8,128)}, u32[]{:S(2)}) copy-start(f32[2,1,96,96]{3,2,1,0:T(8,128)} %get-tuple-element.36) | copy-start | bytes 221188
  77.0 2.8 %copy-start.3 = (f32[2,1,96]{2,1,0:T(1,128)S(1)}, f32[2,1,96]{2,1,0:T(1,128)}, u32[]{:S(2)}) copy-start(f32[2,1,96]{2,1,0:T(1,128)} %get-tuple-element.37) | copy-start | bytes 2308
  77.0 3.3 %copy-start.6 = (f32[1,96]{1,0:T(1,128)S(1)}, f32[1,96]{1,0:T(1,128)}, u32[]{:S(2)}) copy-start(f32[1,96]{1,0:T(1,128)} %get-tuple-element.22) | copy-start | bytes 1156
  77.0 3.8 %copy-start.5 = (f32[1,96]{1,0:T(1,128)S(1)}, f32[1,96]{1,0:T(1,128)}, u32[]{:S(2)}) copy-start(f32[1,96]{1,0:T(1,128)} %get-tuple-element.23) | copy-start | bytes 1156
where the time goes:
time: 81.6 us; the launch traced here: 81.4 us
  Pallas kernels  74.2 us (91%)
  local copies, waits for them, and re-layouts  6.52 us (8%)
    pallas_call x1, Pallas kernels, on_device(): pl.pallas_call(layer, out_shape=(jax.ShapeDtypeStruct(token, BF16), jax.S...  74.2 us
    unnamed x22, local copies, waits for them, and re-layouts  6.52 us

commit v1 on v0

v1 whole, which is shorter than its diff:
```python
import math

import jax
import jax.numpy as jnp
import ml_dtypes
import numpy as np
from jax import lax
from jax.experimental import pallas as pl
from jax.experimental.pallas import tpu as pltpu
from jax.sharding import PartitionSpec as P

C = 768
CB = 96
W = 180
WP = 192
MW = 64
H = 96
NS = 32
NC = 8
HL = H // NS
LN = 128
PL = 5 * LN
HB = 2 * CB

shrink_level = 0.05
norm_epsilon = 1e-05
gelu_scale = 0.7978845608
gelu_cubic = 0.044715
lon_factor = 1.0 / math.sqrt(W)
lat_factor = 1.0 / math.sqrt(H)

F32 = jnp.float32
BF16 = jnp.bfloat16
MESH = pl.DeviceIdType.MESH

RS1, AG1, A2, A1, A4, A3, RS2, AG2 = range(0, 16, 2)
GWR, GWG, GG = range(16, 19)


def twiddle(length, columns):
    rows = np.arange(length)[:, None]
    cols = np.arange(columns)[None, :]
    angles = (rows * cols % length).astype(np.float32) * np.float32(2.0 * math.pi / length)
    return (
        np.cos(angles).astype(np.float32),
        np.sin(angles).astype(np.float32),
    )


def tables():
    bf = ml_dtypes.bfloat16
    cos_lon, sin_lon = (t.astype(bf).astype(np.float32) for t in twiddle(W, MW))
    cos_lat, sin_lat = (t.astype(bf).astype(np.float32) for t in twiddle(H, H))
    lon = np.zeros((NS, 2, 2, 2, 2, WP), np.float32)
    scaled = np.zeros_like(lon)
    for d in range(NS):
        for mm in range(2):
            m = 2 * d + mm
            twice = 1.0 if m == 0 else 2.0
            for b in range(2):
                lon[d, 0, mm, b, b, :W] = cos_lon[:, m]
                lon[d, 1, mm, b, b, :W] = -sin_lon[:, m]
                scaled[d, :, mm, b] = twice * lon[d, :, mm, b]
    lon = lon.reshape(8 * NS, 2 * WP)
    scaled = scaled.reshape(8 * NS, 2 * WP)
    lat = np.zeros((HL, 2, 2, 2, H, NS, 2, 2, 2), np.float32)
    for hh in range(HL):
        cos_part = cos_lat[:, hh::HL]
        sin_part = sin_lat[:, hh::HL]
        for mm in range(2):
            for b in range(2):
                lat[hh, mm, b, 0, :, :, 0, mm, b] = cos_part
                lat[hh, mm, b, 0, :, :, 1, mm, b] = sin_part
                lat[hh, mm, b, 1, :, :, 0, mm, b] = -sin_part
                lat[hh, mm, b, 1, :, :, 1, mm, b] = cos_part
    lat = lat.reshape(HL, 8 * H, 8 * NS)
    return (
        np.stack([lon, scaled]).astype(bf),
        np.stack([lon.T, scaled.T]).astype(bf),
        lat.astype(bf),
        np.swapaxes(lat, 1, 2).astype(bf),
    )


def dot(left, right):
    return lax.dot_general(left, right, (((1,), (0,)), ((), ())), preferred_element_type=F32)


def dot_nt(left, right):
    return lax.dot_general(left, right, (((1,), (1,)), ((), ())), preferred_element_type=F32)


def dot_tn(left, right):
    return lax.dot_general(left, right, (((0,), (0,)), ((), ())), preferred_element_type=F32)


def unpack(source, target, h):
    lane = lax.broadcasted_iota(jnp.int32, (8, LN), 1)

    def step(it, carry):
        for u in range(15):
            i = it * 15 + u
            chunk = source[h, 0, :, pl.ds(pl.multiple_of(i * 384, 128), 384)].astype(F32)
            v0, v1, v2 = chunk[:, :128], chunk[:, 128:256], chunk[:, 256:]
            parts = (
                v0,
                pltpu.roll(jnp.where(lane >= 96, v0, v1), 32, 1),
                pltpu.roll(jnp.where(lane >= 64, v1, v2), 64, 1),
                pltpu.roll(v2, 96, 1),
            )
            for q in range(4):
                target[h, pl.ds(pl.multiple_of(i * 32 + 8 * q, 8), 8), :] = parts[q]
        return carry

    lax.fori_loop(0, 3, step, 0)


def pack(source, target, h):
    lane = lax.broadcasted_iota(jnp.int32, (8, LN), 1)

    def step(it, carry):
        for u in range(15):
            i = it * 15 + u
            p0, p1, p2, p3 = (
                source[h, pl.ds(pl.multiple_of(i * 32 + 8 * q, 8), 8), :] for q in range(4)
            )
            r1 = pltpu.roll(p1, 96, 1)
            r2 = pltpu.roll(p2, 64, 1)
            r3 = pltpu.roll(p3, 32, 1)
            chunk = jnp.concatenate(
                [
                    jnp.where(lane < 96, p0, r1),
                    jnp.where(lane < 64, r1, r2),
                    jnp.where(lane < 32, r2, r3),
                ],
                axis=1,
            )
            target[h, 0, :, pl.ds(pl.multiple_of(i * 384, 128), 384)] = chunk.astype(BF16)
        return carry

    lax.fori_loop(0, 3, step, 0)


def layer(
    x_hbm, cot_hbm, gain_ref, shift_ref, w1_ref, b1_ref, w2_ref, b2_ref,
    d_hbm, e_hbm, l_hbm, m_hbm,
    mixed_out, gin_out, gw1_ref, gb1_ref, gw2_ref, gb2_ref, gg_ref, gs_ref,
    xv, cv, dv, ev, lv, mv, tx, tc, xn, cen, gc,
    send1, send2, send3, send4, recv1, recv2, recv3, recv4,
    lt, gsh, hid, gpost, gpre, sh, glat, wc, vec,
    acc, st, rb, ags, ab, at, acc2, st2, rb2, ags2, ab2, at2,
    gb, gr, gas, ga, ggs, ggr,
    in_sems, send_sems, recv_sems,
):
    me_s = lax.axis_index("space")
    me_c = lax.axis_index("chan")

    loads = [pltpu.make_async_copy(x_hbm.at[h], xv.at[h], in_sems.at[h]) for h in range(HL)]
    loads += [pltpu.make_async_copy(cot_hbm.at[h], cv.at[h], in_sems.at[3 + h]) for h in range(HL)]
    loads += [
        pltpu.make_async_copy(d_hbm, dv, in_sems.at[6]),
        pltpu.make_async_copy(e_hbm, ev, in_sems.at[7]),
        pltpu.make_async_copy(l_hbm, lv, in_sems.at[8]),
        pltpu.make_async_copy(m_hbm, mv, in_sems.at[9]),
    ]
    for load in loads:
        load.start()

    barrier = pltpu.get_barrier_semaphore()

    def greet_space(r, carry):
        pl.semaphore_signal(
            barrier, inc=1, device_id={"space": lax.rem(me_s + r, NS)}, device_id_type=MESH
        )
        return carry

    def greet_chan(r, carry):
        pl.semaphore_signal(
            barrier, inc=1, device_id={"chan": lax.rem(me_c + r, NC)}, device_id_type=MESH
        )
        return carry

    lax.fori_loop(1, NC, greet_chan, 0)
    lax.fori_loop(1, NS, greet_space, 0)

    def spread(axis, index, piece, target):
        count, me = (NS, me_s) if axis == "space" else (NC, me_c)

        def step(r, carry):
            t = lax.rem(me + r, count)
            pltpu.make_async_remote_copy(
                src_ref=piece(t),
                dst_ref=target.at[me],
                send_sem=send_sems.at[index],
                recv_sem=recv_sems.at[index],
                device_id={axis: t},
                device_id_type=MESH,
            ).start()
            return carry

        lax.fori_loop(1, count, step, 0)
        pltpu.make_async_copy(piece(me), target.at[me], recv_sems.at[index]).start()

    def arrived(index, target):
        pltpu.make_async_copy(target, target, recv_sems.at[index]).wait()

    def sent(index, target, count):
        rest = target.at[pl.ds(0, count - 1)]
        pltpu.make_async_copy(rest, rest, send_sems.at[index]).wait()

    vec[...] = jnp.zeros_like(vec)
    vec[0:1, 0:CB] = gain_ref[...]
    vec[1:2, 0:CB] = shift_ref[...]
    for layer_at, (b_ref, w_ref) in enumerate(((b1_ref, w1_ref), (b2_ref, w2_ref))):
        vec[2 + layer_at : 3 + layer_at, 0:CB] = b_ref[0]
        vec[2 + layer_at : 3 + layer_at, LN : LN + CB] = b_ref[1]
        wc[layer_at] = jnp.zeros((2 * LN, 2 * LN), BF16)
        w_real, w_imag = w_ref[0, 0], w_ref[1, 0]
        wc[layer_at, 0:CB, 0:CB] = w_real
        wc[layer_at, 0:CB, LN : LN + CB] = w_imag
        wc[layer_at, LN : LN + CB, 0:CB] = -w_imag
        wc[layer_at, LN : LN + CB, LN : LN + CB] = w_real
    tx[:, 8 * W :, :] = jnp.zeros((HL, 8 * (WP - W), LN), F32)
    tc[:, 8 * W :, :] = jnp.zeros((HL, 8 * (WP - W), LN), F32)
    acc[...] = jnp.zeros_like(acc)
    acc2[...] = jnp.zeros_like(acc2)
    ab[:, NC:] = jnp.zeros((2, NC, 8, LN), F32)
    ab2[:, NC:] = jnp.zeros((2, NC, 8, LN), F32)
    lane_t = lax.broadcasted_iota(jnp.int32, (4 * H, 2 * LN), 1)
    for s in range(2):
        send3[s, :, :, PL - LN :] = jnp.zeros((NS, 8, LN), BF16)
        send4[s, :, :, PL - LN :] = jnp.zeros((NS, 8, LN), BF16)
        for g in range(2):
            lt[s, g] = jnp.where(lane_t == CB, 1.0, 0.0).astype(BF16)
            gsh[s, g] = jnp.zeros((4 * H, 2 * LN), BF16)

    lane_w = lax.broadcasted_iota(jnp.int32, (WP, LN), 1)
    gain_row = vec[0:1, 0:LN]
    shift_row = vec[1:2, 0:LN]

    def members_of(array, h, b):
        return array[h, pl.ds(b, WP, stride=8), :]

    def pair_of(m):
        return m // 2, m % 2

    def dense(tiles):
        t0, t1, t2, t3, t4, t5 = tiles
        r1, r2, r3 = pltpu.roll(t1, 96, 1), pltpu.roll(t2, 64, 1), pltpu.roll(t3, 32, 1)
        r5 = pltpu.roll(t5, 96, 1)
        return (
            jnp.where(lane_w < 96, t0, r1),
            jnp.where(lane_w < 64, r1, r2),
            jnp.where(lane_w < 32, r2, r3),
            jnp.where(lane_w < 96, t4, r5),
            jnp.where(lane_w < 64, r5, 0.0),
        )

    def tile_of(array, h, m):
        pair, one = pair_of(m)
        rows = slice(WP * pair, WP * pair + WP)
        start = HB * h + CB * one
        first, shift = start // LN * LN, start % LN
        left = array[rows, first : first + LN]
        if shift == 0:
            return left
        if shift > 32:
            right = array[rows, first + LN : first + 2 * LN]
            left = jnp.where(lane_w >= shift, left, right)
        return pltpu.roll(left, LN - shift, 1)

    def store_dense(s, pair, tiles):
        for i, column in enumerate(dense(tiles)):
            xn[s, WP * pair : WP * pair + WP, LN * i : LN * i + LN] = column.astype(BF16)

    def pieces_of_sums(source, target):
        turned = jnp.transpose(source[...])
        for part in range(2):
            for m in range(4):
                target[4 * part + m] = turned[8 * m : 8 * m + 8, LN * part : LN * part + LN]

    def columns_of(source, target):
        turned = jnp.transpose(source[...].reshape(LN, LN))
        target[0:LN, 0:32] = turned[:, 0:32]
        target[LN:, 0:32] = turned[:, 32:64]

    for h in range(HL):
        loads[h].wait()
        unpack(xv, tx, h)

    def token_sums(s):
        total = jnp.zeros((WP, LN), F32)
        for m in range(4):
            for h in range(HL):
                tile = jnp.where(lane_w < CB, members_of(tx, h, 4 * s + m), 0.0)
                one = jnp.sum(tile, axis=1, keepdims=True)
                two = jnp.sum(tile * tile, axis=1, keepdims=True)
                total = jnp.where(lane_w == 8 * m + h, one, total)
                total = jnp.where(lane_w == 8 * m + 3 + h, two, total)
        acc[s, 0:WP, :] = total
        pieces_of_sums(acc.at[s], st.at[s])

    token_sums(0)
    pl.semaphore_wait(barrier, NS - 1 + NC - 1)
    spread("chan", RS1, lambda t: st.at[0, t], rb.at[0])
    token_sums(1)
    spread("chan", RS1 + 1, lambda t: st.at[1, t], rb.at[1])

    for h in range(HL):
        loads[3 + h].wait()
        unpack(cv, tc, h)
    loads[6].wait()

    def send_cotangent(s):
        for pair in range(2):
            store_dense(
                s,
                pair,
                [
                    members_of(tc, h, 4 * s + 2 * pair + one)
                    for h in range(HL)
                    for one in range(2)
                ],
            )
        out = dot(dv[1], xn[s]) * lon_factor
        send2[s] = out.reshape(NS, 8, PL).astype(BF16)
        spread("space", A2 + s, lambda t: send2.at[s, t], recv2.at[s])

    def share_statistics(s):
        arrived(RS1 + s, rb.at[s])
        sums = jnp.sum(rb[s], axis=0) * (1.0 / C)
        var_in = pltpu.roll(sums, 5, 0)
        inv = lax.rsqrt(var_in - sums * sums + norm_epsilon)
        row8 = lax.broadcasted_iota(jnp.int32, (8, LN), 0)
        ags[s] = jnp.where(row8 < 3, sums, jnp.where(row8 < 6, pltpu.roll(inv, 3, 0), 0.0))
        spread("chan", AG1 + s, lambda t: ags.at[s], ab.at[s])

    send_cotangent(0)
    share_statistics(0)
    share_statistics(1)
    send_cotangent(1)

    def send_normed(s):
        arrived(AG1 + s, ab.at[s, pl.ds(0, NC)])
        columns_of(ab.at[s], at.at[s])
        for pair in range(2):
            tiles = []
            for h in range(HL):
                for one in range(2):
                    m = 2 * pair + one
                    column = 8 * m + h
                    mean_col = at[s, 0:WP, column : column + 1]
                    inv_col = at[s, 0:WP, column + 3 : column + 4]
                    centred = (members_of(tx, h, 4 * s + m) - mean_col) * inv_col
                    cen[s, 4 * h + m] = centred
                    tiles.append(centred * gain_row + shift_row)
            store_dense(s, pair, tiles)
        out = dot(dv[0], xn[s]) * lon_factor
        send1[s] = out.reshape(NS, 8, PL).astype(BF16)
        spread("space", A1 + s, lambda t: send1.at[s, t], recv1.at[s])

    send_normed(0)
    send_normed(1)

    def latitude(received, target):
        whole = received[...].reshape(8 * NS, PL)
        spectra = [whole[:, HB * h : HB * h + HB] for h in range(HL)]
        for g in range(4):
            rows = slice(2 * H * g, 2 * H * g + 2 * H)
            out = dot(lv[0, rows, :], spectra[0])
            for h in range(1, HL):
                out = out + dot(lv[h, rows, :], spectra[h])
            out = (out * lat_factor).astype(BF16)
            for part in range(2):
                for one in range(2):
                    at_row = HB * (g % 2) + H * one
                    target[g // 2, at_row : at_row + H, LN * part : LN * part + CB] = out[
                        H * part : H * part + H, CB * one : CB * one + CB
                    ]

    loads[8].wait()

    def mix(s):
        def step(i, carry):
            pre = dot(lt[s, i], wc[0]) + vec[2:3, :]
            t = jnp.tanh(gelu_scale * (pre + gelu_cubic * pre * pre * pre))
            hidden = 0.5 * pre * (1.0 + t)
            hidden = jnp.where(lane_t == CB, 1.0, hidden).astype(BF16)
            slope = 0.5 * (1.0 + t) + 0.5 * pre * (1.0 - t * t) * gelu_scale * (
                1.0 + 3.0 * gelu_cubic * pre * pre
            )
            hid[s, i] = hidden
            post = dot(hidden, wc[1]) + vec[3:4, :]
            shape = jnp.tanh(post * (1.0 / shrink_level))
            shrunk = (post - shrink_level * shape).astype(BF16)
            grad_post = (gsh[s, i].astype(F32) * (shape * shape)).astype(BF16)
            gpost[s, i] = grad_post
            grad_pre = (dot_nt(grad_post, wc[1]) * slope).astype(BF16)
            gpre[s, i] = grad_pre
            grad_lat = dot_nt(grad_pre, wc[0]).astype(BF16)
            for pair in range(2):
                for part in range(2):
                    for one in range(2):
                        rows = slice(HB * pair + H * part, HB * pair + H * part + H)
                        lanes = slice(CB * one, CB * one + CB)
                        from_rows = slice(HB * pair + H * one, HB * pair + H * one + H)
                        from_lanes = slice(LN * part, LN * part + CB)
                        sh[s, i, rows, lanes] = shrunk[from_rows, from_lanes]
                        glat[s, i, rows, lanes] = grad_lat[from_rows, from_lanes]
            return carry

        lax.fori_loop(0, 2, step, 0)

    def back(source, target):
        spectrum = source[...].reshape(8 * H, HB)
        for h in range(HL):
            out = dot(mv[h], spectrum) * lat_factor
            target[:, :, HB * h : HB * h + HB] = out.reshape(NS, 8, HB).astype(BF16)

    for s in range(2):
        arrived(A2 + s, recv2.at[s])
        latitude(recv2.at[s], gsh.at[s])
    loads[9].wait()
    for s in range(2):
        arrived(A1 + s, recv1.at[s])
        latitude(recv1.at[s], lt.at[s])
        mix(s)
        back(glat.at[s], send4.at[s])
        spread("space", A4 + s, lambda t, s=s: send4.at[s, t], recv4.at[s])
        back(sh.at[s], send3.at[s])
    for s in range(2):
        spread("space", A3 + s, lambda t, s=s: send3.at[s, t], recv3.at[s])

    for layer_at, (left, right) in enumerate(((lt, gpre), (hid, gpost))):
        outer = dot_tn(left[...].reshape(16 * H, 2 * LN), right[...].reshape(16 * H, 2 * LN))
        real = outer[0:LN, 0:LN] + outer[LN:, LN:]
        imag = outer[0:LN, LN:] - outer[LN:, 0:LN]
        gb[16 * layer_at : 16 * layer_at + 8] = real.reshape(8, 16, LN).astype(BF16)
        gb[16 * layer_at + 8 : 16 * layer_at + 16] = imag.reshape(8, 16, LN).astype(BF16)
    spread("space", GWR, lambda t: gb.at[t], gr)

    loads[7].wait()
    norm_sums = [jnp.zeros((8, LN), F32), jnp.zeros((8, LN), F32)]

    def gradient_sums(s):
        arrived(A4 + s, recv4.at[s])
        out = dot(ev[0], recv4[s].reshape(8 * NS, PL)) * lon_factor
        total = jnp.zeros((WP, LN), F32)
        for h in range(HL):
            for m in range(4):
                grad_normed = tile_of(out, h, m)
                centred = cen[s, 4 * h + m]
                product = grad_normed * centred
                norm_sums[0] = norm_sums[0] + jnp.sum(product.reshape(WP // 8, 8, LN), axis=0)
                norm_sums[1] = norm_sums[1] + jnp.sum(grad_normed.reshape(WP // 8, 8, LN), axis=0)
                grad_centred = grad_normed * gain_row
                gc[s, 4 * h + m] = grad_centred
                one = jnp.sum(grad_centred, axis=1, keepdims=True)
                two = jnp.sum(grad_centred * centred, axis=1, keepdims=True)
                total = jnp.where(lane_w == 8 * m + h, one, total)
                total = jnp.where(lane_w == 8 * m + 3 + h, two, total)
        acc2[s, 0:WP, :] = total
        pieces_of_sums(acc2.at[s], st2.at[s])
        spread("chan", RS2 + s, lambda t: st2.at[s, t], rb2.at[s])

    gradient_sums(0)
    gradient_sums(1)
    ggs[0:1, :] = jnp.sum(norm_sums[0], axis=0, keepdims=True)
    ggs[1:2, :] = jnp.sum(norm_sums[1], axis=0, keepdims=True)
    spread("space", GG, lambda t: ggs, ggr)

    def share_gradient_sums(s):
        arrived(RS2 + s, rb2.at[s])
        ags2[s] = jnp.sum(rb2[s], axis=0) * (1.0 / C)
        spread("chan", AG2 + s, lambda t: ags2.at[s], ab2.at[s])

    share_gradient_sums(0)
    arrived(GWR, gr)
    gas[...] = jnp.sum(gr[...].astype(F32), axis=0).astype(BF16)
    spread("space", GWG, lambda t: gas, ga)
    share_gradient_sums(1)

    def put_mixed(s):
        arrived(A3 + s, recv3.at[s])
        out = dot(ev[1], recv3[s].reshape(8 * NS, PL)) * lon_factor
        for h in range(HL):
            for m in range(4):
                put_members(tc, h, 4 * s + m, tile_of(out, h, m))

    def put_members(array, h, b, tile):
        array[h, pl.ds(b, WP, stride=8), :] = tile

    def put_gradient(s):
        arrived(AG2 + s, ab2.at[s, pl.ds(0, NC)])
        columns_of(ab2.at[s], at2.at[s])
        for h in range(HL):
            for m in range(4):
                column = 8 * m + h
                inv_col = at[s, 0:WP, column + 3 : column + 4]
                first = at2[s, 0:WP, column : column + 1]
                second = at2[s, 0:WP, column + 3 : column + 4]
                put_members(
                    tx,
                    h,
                    4 * s + m,
                    inv_col * (gc[s, 4 * h + m] - first - cen[s, 4 * h + m] * second),
                )

    put_mixed(0)
    put_gradient(0)
    put_gradient(1)
    for h in range(HL):
        pack(tx, gin_out, h)
    put_mixed(1)
    for h in range(HL):
        pack(tc, mixed_out, h)

    arrived(GG, ggr)
    both = jnp.sum(ggr[...], axis=0)
    gg_ref[...] = both[0:1, 0:CB]
    gs_ref[...] = both[1:2, 0:CB]
    arrived(GWG, ga)
    for layer_at, (gw_ref, gbias_ref) in enumerate(((gw1_ref, gb1_ref), (gw2_ref, gb2_ref))):
        for part in range(2):
            at_piece = 16 * layer_at + 8 * part
            block = ga[at_piece : at_piece + 8].astype(F32).reshape(LN, LN)
            gw_ref[part, 0] = block[0:CB, 0:CB]
            gbias_ref[part] = block[CB : CB + 1, 0:CB]

    for s in range(2):
        sent(RS1 + s, rb.at[s], NC)
        sent(AG1 + s, ab.at[s], NC)
        sent(RS2 + s, rb2.at[s], NC)
        sent(AG2 + s, ab2.at[s], NC)
        sent(A2 + s, recv2.at[s], NS)
        sent(A1 + s, recv1.at[s], NS)
        sent(A4 + s, recv4.at[s], NS)
        sent(A3 + s, recv3.at[s], NS)
    sent(GWR, gr, NS)
    sent(GWG, ga, NS)
    sent(GG, ggr, NS)


def write_out(*refs):
    count = (len(refs) - 1) // 2
    sems = refs[-1]
    copies = [
        pltpu.make_async_copy(refs[i], refs[count + i], sems.at[i]) for i in range(count)
    ]
    for copy in copies:
        copy.start()
    for copy in copies:
        copy.wait()


def on_device(members, gain, shift, w_first, b_first, w_second, b_second, cotangent):
    lon_out, lon_back, lat_out, lat_back = (jnp.asarray(t) for t in tables())
    anywhere = pl.BlockSpec(memory_space=pl.ANY)
    vmem = pl.BlockSpec(memory_space=pltpu.VMEM)
    token = (HL, 1, 8, W * CB)
    piece = (2, NS, 8, PL)
    spectral = (2, 2, 4 * H, 2 * LN)
    folded = (2, 2, 4 * H, HB)
    results = (
        jax.ShapeDtypeStruct(token, BF16),
        jax.ShapeDtypeStruct(token, BF16),
        jax.ShapeDtypeStruct((2, 1, CB, CB), F32),
        jax.ShapeDtypeStruct((2, 1, CB), F32),
        jax.ShapeDtypeStruct((2, 1, CB, CB), F32),
        jax.ShapeDtypeStruct((2, 1, CB), F32),
        jax.ShapeDtypeStruct((1, CB), F32),
        jax.ShapeDtypeStruct((1, CB), F32),
    )
    outs = pl.pallas_call(
        layer,
        out_shape=tuple(pltpu.VMEM(r.shape, r.dtype) for r in results),
        in_specs=[anywhere] * 2 + [vmem] * 6 + [anywhere] * 4,
        out_specs=tuple([vmem] * 8),
        scratch_shapes=[
            pltpu.VMEM(token, BF16),
            pltpu.VMEM(token, BF16),
            pltpu.VMEM((2, 8 * NS, 2 * WP), BF16),
            pltpu.VMEM((2, 2 * WP, 8 * NS), BF16),
            pltpu.VMEM((HL, 8 * H, 8 * NS), BF16),
            pltpu.VMEM((HL, 8 * NS, 8 * H), BF16),
            pltpu.VMEM((HL, 8 * WP, LN), F32),
            pltpu.VMEM((HL, 8 * WP, LN), F32),
            pltpu.VMEM((2, 2 * WP, PL), BF16),
            pltpu.VMEM((2, 4 * HL, WP, LN), F32),
            pltpu.VMEM((2, 4 * HL, WP, LN), F32),
        ]
        + [pltpu.VMEM(piece, BF16)] * 8
        + [pltpu.VMEM(spectral, BF16)] * 5
        + [pltpu.VMEM(folded, BF16)] * 2
        + [
            pltpu.VMEM((2, 2 * LN, 2 * LN), BF16),
            pltpu.VMEM((8, 2 * LN), F32),
        ]
        + [
            pltpu.VMEM((2, 2 * LN, LN), F32),
            pltpu.VMEM((2, NC, 8, LN), F32),
            pltpu.VMEM((2, NC, 8, LN), F32),
            pltpu.VMEM((2, 8, LN), F32),
            pltpu.VMEM((2, 2 * NC, 8, LN), F32),
            pltpu.VMEM((2, 2 * LN, LN), F32),
        ]
        * 2
        + [
            pltpu.VMEM((NS, 16, LN), BF16),
            pltpu.VMEM((NS, 16, LN), BF16),
            pltpu.VMEM((16, LN), BF16),
            pltpu.VMEM((NS, 16, LN), BF16),
            pltpu.VMEM((2, LN), F32),
            pltpu.VMEM((NS, 2, LN), F32),
            pltpu.SemaphoreType.DMA((10,)),
            pltpu.SemaphoreType.DMA((19,)),
            pltpu.SemaphoreType.DMA((19,)),
        ],
        compiler_params=pltpu.CompilerParams(
            collective_id=0, has_side_effects=True, vmem_limit_bytes=52 * 1024 * 1024
        ),
    )(
        jnp.transpose(members, (1, 2, 0, 3)),
        jnp.transpose(cotangent, (1, 2, 0, 3)),
        gain.reshape(1, CB),
        shift.reshape(1, CB),
        w_first,
        b_first,
        w_second,
        b_second,
        lon_out,
        lon_back,
        lat_out,
        lat_back,
    )
    outs = [pltpu.with_memory_space_constraint(o, pltpu.VMEM) for o in outs]
    mixed, grad_input, gw1, gb1, gw2, gb2, gg, gs = pl.pallas_call(
        write_out,
        out_shape=results,
        in_specs=[vmem] * 8,
        out_specs=tuple([anywhere] * 8),
        scratch_shapes=[pltpu.SemaphoreType.DMA((8,))],
    )(*outs)
    return (
        jnp.transpose(mixed, (2, 0, 1, 3)),
        jnp.transpose(grad_input, (2, 0, 1, 3)),
        gw1,
        gb1,
        gw2,
        gb2,
        gg.reshape(CB),
        gs.reshape(CB),
    )


def solution(mesh):
    placed = (
        P(None, "space", "chan", None),
        P("chan"),
        P("chan"),
        P(None, "chan", None, None),
        P(None, "chan", None),
        P(None, "chan", None, None),
        P(None, "chan", None),
        P(None, "space", "chan", None),
    )
    return jax.shard_map(
        on_device,
        mesh=mesh,
        in_specs=placed,
        out_specs=(
            P(None, "space", "chan", None),
            P(None, "space", "chan", None),
            P(None, "chan", None, None),
            P(None, "chan", None),
            P(None, "chan", None, None),
            P(None, "chan", None),
            P("chan"),
            P("chan"),
        ),
        check_vma=False,
    )
```

time: 81.6 us -> 66.8 us (0.82)
  Pallas kernels: 74.2 us -> 61.4 us
  local copies, waits for them, and re-layouts: 6.52 us -> 4.26 us
    pallas_call x1 -> x2, Pallas kernels: 74.2 us -> 61.4 us  [the longest x1 60.1 us: on_device(): pl.pallas_call(layer, out_shape=tuple((pltpu.VMEM(r.shape, r.dtype) for r...]
    unnamed x22 -> x12, local copies, waits for them, and re-layouts: 6.52 us -> 4.26 us
where the time goes in v1:
time: 66.8 us; the launch traced here: 66.5 us
  Pallas kernels  61.4 us (92%)
  local copies, waits for them, and re-layouts  4.26 us (6%)
  between operations  0.82 us (1%)
    pallas_call x1, Pallas kernels, on_device(): pl.pallas_call(layer, out_shape=tuple((pltpu.VMEM(r.shape, r.dtype) for r...  60.1 us
    unnamed x12, local copies, waits for them, and re-layouts  4.26 us

profile of v1, /device:TPU:1, one launch (start us, length us, event | category | flops | bytes accessed | tf_op | source)
XLA Modules:
  0.0 66.5 jit_solution(15658785988959922364)
XLA Ops:
  0.6 0.0 copy-start
  0.6 0.8 %copy-done = bf16[2,1,96,96]{3,2,1,0:T(8,128)(2,1)S(1)} copy-done((bf16[2,1,96,96]{3,2,1,0:T(8,128)(2,1)S(1)}, bf16[2,1,96,96]{3,2,1,0:T(8,128)(2,1)}, u32[]{:S(2)}) %copy-start) | copy-done | bytes 36888
  1.4 0.0 copy-start.1
  1.4 0.8 %copy-done.1 = bf16[2,1,96,96]{3,2,1,0:T(8,128)(2,1)S(1)} copy-done((bf16[2,1,96,96]{3,2,1,0:T(8,128)(2,1)S(1)}, bf16[2,1,96,96]{3,2,1,0:T(8,128)(2,1)}, u32[]{:S(2)}) %copy-start.1) | copy-done | bytes 36888
  2.2 0.0 copy-start.2
  2.2 0.7 %copy-done.2 = f32[2,1,96]{2,1,0:T(1,128)S(1)} copy-done((f32[2,1,96]{2,1,0:T(1,128)S(1)}, f32[2,1,96]{2,1,0:T(1,128)}, u32[]{:S(2)}) %copy-start.2) | copy-done | bytes 792
  2.9 0.0 copy-start.3
  2.9 0.7 %copy-done.3 = f32[2,1,96]{2,1,0:T(1,128)S(1)} copy-done((f32[2,1,96]{2,1,0:T(1,128)S(1)}, f32[2,1,96]{2,1,0:T(1,128)}, u32[]{:S(2)}) %copy-start.3) | copy-done | bytes 792
  3.6 0.0 copy-start.4
  3.6 0.7 copy-done.4
  4.2 0.0 copy-start.5
  4.3 0.7 copy-done.5
  4.9 60.1 %shard_map.179 = (bf16[3,1,8,17280]{3,2,1,0:T(8,128)(2,1)S(1)}, bf16[3,1,8,17280]{3,2,1,0:T(8,128)(2,1)S(1)}, f32[2,1,96,96]{3,2,1,0:T(8,128)S(1)}, f32[2,1,96]{...) custom-call(bf16[3,1,8,17280]{3,2,1,0:T(8,128)(2,1)} %bitcast.10, ...), custom_call_target="tpu_custom_call" | custom-call | tf_op jit(solution)/shard_map/pallas_call | solution.py:574
  65.0 1.3 %shard_map.180 = (bf16[3,1,8,17280]{3,2,1,0:T(8,128)(2,1)}, bf16[3,1,8,17280]{3,2,1,0:T(8,128)(2,1)}, f32[2,1,96,96]{3,2,1,0:T(8,128)}, f32[2,1,96]{2,1,0:T(1,12...) custom-call(bf16[3,1,8,17280]{3,2,1,0:T(8,128)(2,1)S(1)} %get-tuple-element.24.refs_0_, ...), custom_call_target="tpu_custom_call" | custom-call | tf_op jit(solution)/shard_map/pallas_call | solution.py:637
Async XLA Ops:
  0.6 0.8 %copy-start = (bf16[2,1,96,96]{3,2,1,0:T(8,128)(2,1)S(1)}, bf16[2,1,96,96]{3,2,1,0:T(8,128)(2,1)}, u32[]{:S(2)}) copy-start(bf16[2,1,96,96]{3,2,1,0:T(8,128)(2,1)} %w1_ref.1) | copy-start | bytes 110596
  1.4 0.8 %copy-start.1 = (bf16[2,1,96,96]{3,2,1,0:T(8,128)(2,1)S(1)}, bf16[2,1,96,96]{3,2,1,0:T(8,128)(2,1)}, u32[]{:S(2)}) copy-start(bf16[2,1,96,96]{3,2,1,0:T(8,128)(2,1)} %w2_ref.1) | copy-start | bytes 110596
  2.2 0.7 %copy-start.2 = (f32[2,1,96]{2,1,0:T(1,128)S(1)}, f32[2,1,96]{2,1,0:T(1,128)}, u32[]{:S(2)}) copy-start(f32[2,1,96]{2,1,0:T(1,128)} %b1_ref.1) | copy-start | bytes 2308
  2.9 0.7 %copy-start.3 = (f32[2,1,96]{2,1,0:T(1,128)S(1)}, f32[2,1,96]{2,1,0:T(1,128)}, u32[]{:S(2)}) copy-start(f32[2,1,96]{2,1,0:T(1,128)} %b2_ref.1) | copy-start | bytes 2308
  3.6 0.7 copy-start.4
  4.2 0.7 copy-start.5

commit v2 on v1

--- a/solution.py
+++ b/solution.py
@@ -142,14 +142,14 @@
 
 
 def layer(
-    x_hbm, cot_hbm, gain_ref, shift_ref, w1_ref, b1_ref, w2_ref, b2_ref,
+    x_hbm, cot_hbm, gain_hbm, shift_hbm, w1_hbm, b1_hbm, w2_hbm, b2_hbm,
     d_hbm, e_hbm, l_hbm, m_hbm,
     mixed_out, gin_out, gw1_ref, gb1_ref, gw2_ref, gb2_ref, gg_ref, gs_ref,
     xv, cv, dv, ev, lv, mv, tx, tc, xn, cen, gc,
     send1, send2, send3, send4, recv1, recv2, recv3, recv4,
     lt, gsh, hid, gpost, gpre, sh, glat, wc, vec,
     acc, st, rb, ags, ab, at, acc2, st2, rb2, ags2, ab2, at2,
-    gb, gr, gas, ga, ggs, ggr,
+    gb, gr, gas, ga, ggs, ggr, small, w1_v, w2_v, b1_v, b2_v,
     in_sems, send_sems, recv_sems,
 ):
     me_s = lax.axis_index("space")
@@ -162,6 +162,12 @@
         pltpu.make_async_copy(e_hbm, ev, in_sems.at[7]),
         pltpu.make_async_copy(l_hbm, lv, in_sems.at[8]),
         pltpu.make_async_copy(m_hbm, mv, in_sems.at[9]),
+        pltpu.make_async_copy(gain_hbm, small.at[0], in_sems.at[10]),
+        pltpu.make_async_copy(shift_hbm, small.at[1], in_sems.at[11]),
+        pltpu.make_async_copy(w1_hbm, w1_v, in_sems.at[12]),
+        pltpu.make_async_copy(b1_hbm, b1_v, in_sems.at[13]),
+        pltpu.make_async_copy(w2_hbm, w2_v, in_sems.at[14]),
+        pltpu.make_async_copy(b2_hbm, b2_v, in_sems.at[15]),
     ]
     for load in loads:
         load.start()
@@ -208,18 +214,6 @@
         rest = target.at[pl.ds(0, count - 1)]
         pltpu.make_async_copy(rest, rest, send_sems.at[index]).wait()
 
-    vec[...] = jnp.zeros_like(vec)
-    vec[0:1, 0:CB] = gain_ref[...]
-    vec[1:2, 0:CB] = shift_ref[...]
-    for layer_at, (b_ref, w_ref) in enumerate(((b1_ref, w1_ref), (b2_ref, w2_ref))):
-        vec[2 + layer_at : 3 + layer_at, 0:CB] = b_ref[0]
-        vec[2 + layer_at : 3 + layer_at, LN : LN + CB] = b_ref[1]
-        wc[layer_at] = jnp.zeros((2 * LN, 2 * LN), BF16)
-        w_real, w_imag = w_ref[0, 0], w_ref[1, 0]
-        wc[layer_at, 0:CB, 0:CB] = w_real
-        wc[layer_at, 0:CB, LN : LN + CB] = w_imag
-        wc[layer_at, LN : LN + CB, 0:CB] = -w_imag
-        wc[layer_at, LN : LN + CB, LN : LN + CB] = w_real
     tx[:, 8 * W :, :] = jnp.zeros((HL, 8 * (WP - W), LN), F32)
     tc[:, 8 * W :, :] = jnp.zeros((HL, 8 * (WP - W), LN), F32)
     acc[...] = jnp.zeros_like(acc)
@@ -235,8 +229,6 @@
             gsh[s, g] = jnp.zeros((4 * H, 2 * LN), BF16)
 
     lane_w = lax.broadcasted_iota(jnp.int32, (WP, LN), 1)
-    gain_row = vec[0:1, 0:LN]
-    shift_row = vec[1:2, 0:LN]
 
     def members_of(array, h, b):
         return array[h, pl.ds(b, WP, stride=8), :]
@@ -305,6 +297,23 @@
     spread("chan", RS1, lambda t: st.at[0, t], rb.at[0])
     token_sums(1)
     spread("chan", RS1 + 1, lambda t: st.at[1, t], rb.at[1])
+
+    for k in range(10, 16):
+        loads[k].wait()
+    vec[...] = jnp.zeros_like(vec)
+    vec[0:1, 0:CB] = small[0]
+    vec[1:2, 0:CB] = small[1]
+    for layer_at, (b_ref, w_ref) in enumerate(((b1_v, w1_v), (b2_v, w2_v))):
+        vec[2 + layer_at : 3 + layer_at, 0:CB] = b_ref[0]
+        vec[2 + layer_at : 3 + layer_at, LN : LN + CB] = b_ref[1]
+        wc[layer_at] = jnp.zeros((2 * LN, 2 * LN), BF16)
+        w_real, w_imag = w_ref[0, 0], w_ref[1, 0]
+        wc[layer_at, 0:CB, 0:CB] = w_real
+        wc[layer_at, 0:CB, LN : LN + CB] = w_imag
+        wc[layer_at, LN : LN + CB, 0:CB] = -w_imag
+        wc[layer_at, LN : LN + CB, LN : LN + CB] = w_real
+    gain_row = vec[0:1, 0:LN]
+    shift_row = vec[1:2, 0:LN]
 
     for h in range(HL):
         loads[3 + h].wait()
@@ -427,9 +436,9 @@
         mix(s)
         back(glat.at[s], send4.at[s])
         spread("space", A4 + s, lambda t, s=s: send4.at[s, t], recv4.at[s])
+        if s == 1:
+            spread("space", A3, lambda t: send3.at[0, t], recv3.at[0])
         back(sh.at[s], send3.at[s])
-    for s in range(2):
-        spread("space", A3 + s, lambda t, s=s: send3.at[s, t], recv3.at[s])
 
     for layer_at, (left, right) in enumerate(((lt, gpre), (hid, gpost))):
         outer = dot_tn(left[...].reshape(16 * H, 2 * LN), right[...].reshape(16 * H, 2 * LN))
@@ -438,6 +447,7 @@
         gb[16 * layer_at : 16 * layer_at + 8] = real.reshape(8, 16, LN).astype(BF16)
         gb[16 * layer_at + 8 : 16 * layer_at + 16] = imag.reshape(8, 16, LN).astype(BF16)
     spread("space", GWR, lambda t: gb.at[t], gr)
+    spread("space", A3 + 1, lambda t: send3.at[1, t], recv3.at[1])
 
     loads[7].wait()
     norm_sums = [jnp.zeros((8, LN), F32), jnp.zeros((8, LN), F32)]
@@ -465,9 +475,6 @@
 
     gradient_sums(0)
     gradient_sums(1)
-    ggs[0:1, :] = jnp.sum(norm_sums[0], axis=0, keepdims=True)
-    ggs[1:2, :] = jnp.sum(norm_sums[1], axis=0, keepdims=True)
-    spread("space", GG, lambda t: ggs, ggr)
 
     def share_gradient_sums(s):
         arrived(RS2 + s, rb2.at[s])
@@ -475,10 +482,9 @@
         spread("chan", AG2 + s, lambda t: ags2.at[s], ab2.at[s])
 
     share_gradient_sums(0)
-    arrived(GWR, gr)
-    gas[...] = jnp.sum(gr[...].astype(F32), axis=0).astype(BF16)
-    spread("space", GWG, lambda t: gas, ga)
-    share_gradient_sums(1)
+    ggs[0:1, :] = jnp.sum(norm_sums[0], axis=0, keepdims=True)
+    ggs[1:2, :] = jnp.sum(norm_sums[1], axis=0, keepdims=True)
+    spread("space", GG, lambda t: ggs, ggr)
 
     def put_mixed(s):
         arrived(A3 + s, recv3.at[s])
@@ -507,7 +513,11 @@
                 )
 
     put_mixed(0)
+    share_gradient_sums(1)
     put_gradient(0)
+    arrived(GWR, gr)
+    gas[...] = jnp.sum(gr[...].astype(F32), axis=0).astype(BF16)
+    spread("space", GWG, lambda t: gas, ga)
     put_gradient(1)
     for h in range(HL):
         pack(tx, gin_out, h)
@@ -557,6 +567,7 @@
     lon_out, lon_back, lat_out, lat_back = (jnp.asarray(t) for t in tables())
     anywhere = pl.BlockSpec(memory_space=pl.ANY)
     vmem = pl.BlockSpec(memory_space=pltpu.VMEM)
+    stays = pl.BlockSpec(memory_space=pltpu.HBM)
     token = (HL, 1, 8, W * CB)
     piece = (2, NS, 8, PL)
     spectral = (2, 2, 4 * H, 2 * LN)
@@ -574,7 +585,7 @@
     outs = pl.pallas_call(
         layer,
         out_shape=tuple(pltpu.VMEM(r.shape, r.dtype) for r in results),
-        in_specs=[anywhere] * 2 + [vmem] * 6 + [anywhere] * 4,
+        in_specs=[stays] * 12,
         out_specs=tuple([vmem] * 8),
         scratch_shapes=[
             pltpu.VMEM(token, BF16),
@@ -612,12 +623,17 @@
             pltpu.VMEM((NS, 16, LN), BF16),
             pltpu.VMEM((2, LN), F32),
             pltpu.VMEM((NS, 2, LN), F32),
-            pltpu.SemaphoreType.DMA((10,)),
+            pltpu.VMEM((2, 1, CB), F32),
+            pltpu.VMEM((2, 1, CB, CB), BF16),
+            pltpu.VMEM((2, 1, CB, CB), BF16),
+            pltpu.VMEM((2, 1, CB), F32),
+            pltpu.VMEM((2, 1, CB), F32),
+            pltpu.SemaphoreType.DMA((16,)),
             pltpu.SemaphoreType.DMA((19,)),
             pltpu.SemaphoreType.DMA((19,)),
         ],
         compiler_params=pltpu.CompilerParams(
-            collective_id=0, has_side_effects=True, vmem_limit_bytes=52 * 1024 * 1024
+            collective_id=0, has_side_effects=True, vmem_limit_bytes=60 * 1024 * 1024
         ),
     )(
         jnp.transpose(members, (1, 2, 0, 3)),

time: 66.8 us -> 59.7 us (0.89)
  local copies, waits for them, and re-layouts: 4.26 us -> 0 us
  Pallas kernels: 61.4 us -> 58.8 us
    unnamed x12 -> x0, local copies, waits for them, and re-layouts: 4.26 us -> none
    pallas_call x1, Pallas kernels: 60.1 us -> 57.5 us  [on_device(): pl.pallas_call(layer, out_shape=tuple((pltpu.VMEM(r.shape, r.dtype) for r...]
where the time goes in v2:
time: 59.7 us; the launch traced here: 59.6 us
  Pallas kernels  58.8 us (98%)
  between operations  0.8 us (1%)
    pallas_call x1, Pallas kernels, on_device(): pl.pallas_call(layer, out_shape=tuple((pltpu.VMEM(r.shape, r.dtype) for r...  57.5 us
    pallas_call x1, Pallas kernels, on_device(): pl.pallas_call(write_out, out_shape=results, in_specs=[vmem] * 8, out_spe...  1.3 us

profile of v2, /device:TPU:1, one launch (start us, length us, event | category | flops | bytes accessed | tf_op | source)
XLA Modules:
  0.0 59.6 jit_solution(4915074327743323269)
XLA Ops:
  0.6 57.5 %shard_map.179 = (bf16[3,1,8,17280]{3,2,1,0:T(8,128)(2,1)S(1)}, bf16[3,1,8,17280]{3,2,1,0:T(8,128)(2,1)S(1)}, f32[2,1,96,96]{3,2,1,0:T(8,128)S(1)}, f32[2,1,96]{...) custom-call(bf16[3,1,8,17280]{3,2,1,0:T(8,128)(2,1)} %bitcast.8, ...), custom_call_target="tpu_custom_call" | custom-call | tf_op jit(solution)/shard_map/pallas_call | solution.py:585
  58.1 1.3 %shard_map.180 = (bf16[3,1,8,17280]{3,2,1,0:T(8,128)(2,1)}, bf16[3,1,8,17280]{3,2,1,0:T(8,128)(2,1)}, f32[2,1,96,96]{3,2,1,0:T(8,128)}, f32[2,1,96]{2,1,0:T(1,12...) custom-call(bf16[3,1,8,17280]{3,2,1,0:T(8,128)(2,1)S(1)} %get-tuple-element.24.refs_0_, ...), custom_call_target="tpu_custom_call" | custom-call | tf_op jit(solution)/shard_map/pallas_call | solution.py:653

commit v3 on v2

--- a/solution.py
+++ b/solution.py
@@ -19,8 +19,8 @@
 NC = 8
 HL = H // NS
 LN = 128
-PL = 5 * LN
-HB = 2 * CB
+PL = 9 * LN
+HB = 4 * CB
 
 shrink_level = 0.05
 norm_epsilon = 1e-05
@@ -51,34 +51,31 @@
     bf = ml_dtypes.bfloat16
     cos_lon, sin_lon = (t.astype(bf).astype(np.float32) for t in twiddle(W, MW))
     cos_lat, sin_lat = (t.astype(bf).astype(np.float32) for t in twiddle(H, H))
-    lon = np.zeros((NS, 2, 2, 2, 2, WP), np.float32)
+    lon = np.zeros((NS, 2, 2, WP), np.float32)
     scaled = np.zeros_like(lon)
     for d in range(NS):
         for mm in range(2):
             m = 2 * d + mm
-            twice = 1.0 if m == 0 else 2.0
-            for b in range(2):
-                lon[d, 0, mm, b, b, :W] = cos_lon[:, m]
-                lon[d, 1, mm, b, b, :W] = -sin_lon[:, m]
-                scaled[d, :, mm, b] = twice * lon[d, :, mm, b]
-    lon = lon.reshape(8 * NS, 2 * WP)
-    scaled = scaled.reshape(8 * NS, 2 * WP)
-    lat = np.zeros((HL, 2, 2, 2, H, NS, 2, 2, 2), np.float32)
+            lon[d, 0, mm, :W] = cos_lon[:, m]
+            lon[d, 1, mm, :W] = -sin_lon[:, m]
+            scaled[d, :, mm] = (1.0 if m == 0 else 2.0) * lon[d, :, mm]
+    lon = lon.reshape(4 * NS, WP)
+    scaled = scaled.reshape(4 * NS, WP)
+    lat = np.zeros((2, 2, H, HL, NS, 2, 2), np.float32)
     for hh in range(HL):
         cos_part = cos_lat[:, hh::HL]
         sin_part = sin_lat[:, hh::HL]
         for mm in range(2):
-            for b in range(2):
-                lat[hh, mm, b, 0, :, :, 0, mm, b] = cos_part
-                lat[hh, mm, b, 0, :, :, 1, mm, b] = sin_part
-                lat[hh, mm, b, 1, :, :, 0, mm, b] = -sin_part
-                lat[hh, mm, b, 1, :, :, 1, mm, b] = cos_part
-    lat = lat.reshape(HL, 8 * H, 8 * NS)
+            lat[mm, 0, :, hh, :, 0, mm] = cos_part
+            lat[mm, 0, :, hh, :, 1, mm] = sin_part
+            lat[mm, 1, :, hh, :, 0, mm] = -sin_part
+            lat[mm, 1, :, hh, :, 1, mm] = cos_part
+    lat = lat.reshape(4 * H, 4 * H)
     return (
         np.stack([lon, scaled]).astype(bf),
         np.stack([lon.T, scaled.T]).astype(bf),
         lat.astype(bf),
-        np.swapaxes(lat, 1, 2).astype(bf),
+        lat.T.astype(bf),
     )
 
 
@@ -147,7 +144,7 @@
     mixed_out, gin_out, gw1_ref, gb1_ref, gw2_ref, gb2_ref, gg_ref, gs_ref,
     xv, cv, dv, ev, lv, mv, tx, tc, xn, cen, gc,
     send1, send2, send3, send4, recv1, recv2, recv3, recv4,
-    lt, gsh, hid, gpost, gpre, sh, glat, wc, vec,
+    rc, lt, gsh, hid, gpost, gpre, sh, glat, wc, vec,
     acc, st, rb, ags, ab, at, acc2, st2, rb2, ags2, ab2, at2,
     gb, gr, gas, ga, ggs, ggr, small, w1_v, w2_v, b1_v, b2_v,
     in_sems, send_sems, recv_sems,
@@ -221,49 +218,34 @@
     ab[:, NC:] = jnp.zeros((2, NC, 8, LN), F32)
     ab2[:, NC:] = jnp.zeros((2, NC, 8, LN), F32)
     lane_t = lax.broadcasted_iota(jnp.int32, (4 * H, 2 * LN), 1)
-    for s in range(2):
-        send3[s, :, :, PL - LN :] = jnp.zeros((NS, 8, LN), BF16)
-        send4[s, :, :, PL - LN :] = jnp.zeros((NS, 8, LN), BF16)
-        for g in range(2):
-            lt[s, g] = jnp.where(lane_t == CB, 1.0, 0.0).astype(BF16)
-            gsh[s, g] = jnp.zeros((4 * H, 2 * LN), BF16)
-
+    lane_h = lax.broadcasted_iota(jnp.int32, (H, LN), 1)
     lane_w = lax.broadcasted_iota(jnp.int32, (WP, LN), 1)
 
     def members_of(array, h, b):
         return array[h, pl.ds(b, WP, stride=8), :]
 
-    def pair_of(m):
-        return m // 2, m % 2
-
-    def dense(tiles):
-        t0, t1, t2, t3, t4, t5 = tiles
-        r1, r2, r3 = pltpu.roll(t1, 96, 1), pltpu.roll(t2, 64, 1), pltpu.roll(t3, 32, 1)
-        r5 = pltpu.roll(t5, 96, 1)
+    def dense(tiles, lane):
+        r1, r2, r3 = (pltpu.roll(tiles[i], LN - 32 * i, 1) for i in range(1, 4))
         return (
-            jnp.where(lane_w < 96, t0, r1),
-            jnp.where(lane_w < 64, r1, r2),
-            jnp.where(lane_w < 32, r2, r3),
-            jnp.where(lane_w < 96, t4, r5),
-            jnp.where(lane_w < 64, r5, 0.0),
+            jnp.where(lane < 96, tiles[0], r1),
+            jnp.where(lane < 64, r1, r2),
+            jnp.where(lane < 32, r2, r3),
         )
 
-    def tile_of(array, h, m):
-        pair, one = pair_of(m)
-        rows = slice(WP * pair, WP * pair + WP)
-        start = HB * h + CB * one
+    def tile_of(array, rows, h, m, lane):
+        start = HB * h + CB * m
         first, shift = start // LN * LN, start % LN
         left = array[rows, first : first + LN]
         if shift == 0:
             return left
         if shift > 32:
             right = array[rows, first + LN : first + 2 * LN]
-            left = jnp.where(lane_w >= shift, left, right)
+            left = jnp.where(lane >= shift, left, right)
         return pltpu.roll(left, LN - shift, 1)
 
-    def store_dense(s, pair, tiles):
-        for i, column in enumerate(dense(tiles)):
-            xn[s, WP * pair : WP * pair + WP, LN * i : LN * i + LN] = column.astype(BF16)
+    def store_dense(s, h, tiles):
+        for i, column in enumerate(dense(tiles, lane_w)):
+            xn[s, :, HB * h + LN * i : HB * h + LN * i + LN] = column.astype(BF16)
 
     def pieces_of_sums(source, target):
         turned = jnp.transpose(source[...])
@@ -321,18 +303,10 @@
     loads[6].wait()
 
     def send_cotangent(s):
-        for pair in range(2):
-            store_dense(
-                s,
-                pair,
-                [
-                    members_of(tc, h, 4 * s + 2 * pair + one)
-                    for h in range(HL)
-                    for one in range(2)
-                ],
-            )
+        for h in range(HL):
+            store_dense(s, h, [members_of(tc, h, 4 * s + m) for m in range(4)])
         out = dot(dv[1], xn[s]) * lon_factor
-        send2[s] = out.reshape(NS, 8, PL).astype(BF16)
+        send2[s] = out.reshape(NS, 4, PL).astype(BF16)
         spread("space", A2 + s, lambda t: send2.at[s, t], recv2.at[s])
 
     def share_statistics(s):
@@ -352,40 +326,35 @@
     def send_normed(s):
         arrived(AG1 + s, ab.at[s, pl.ds(0, NC)])
         columns_of(ab.at[s], at.at[s])
-        for pair in range(2):
+        for h in range(HL):
             tiles = []
-            for h in range(HL):
-                for one in range(2):
-                    m = 2 * pair + one
-                    column = 8 * m + h
-                    mean_col = at[s, 0:WP, column : column + 1]
-                    inv_col = at[s, 0:WP, column + 3 : column + 4]
-                    centred = (members_of(tx, h, 4 * s + m) - mean_col) * inv_col
-                    cen[s, 4 * h + m] = centred
-                    tiles.append(centred * gain_row + shift_row)
-            store_dense(s, pair, tiles)
+            for m in range(4):
+                column = 8 * m + h
+                mean_col = at[s, 0:WP, column : column + 1]
+                inv_col = at[s, 0:WP, column + 3 : column + 4]
+                centred = (members_of(tx, h, 4 * s + m) - mean_col) * inv_col
+                cen[s, 4 * h + m] = centred
+                tiles.append(centred * gain_row + shift_row)
+            store_dense(s, h, tiles)
         out = dot(dv[0], xn[s]) * lon_factor
-        send1[s] = out.reshape(NS, 8, PL).astype(BF16)
+        send1[s] = out.reshape(NS, 4, PL).astype(BF16)
         spread("space", A1 + s, lambda t: send1.at[s, t], recv1.at[s])
 
     send_normed(0)
     send_normed(1)
 
-    def latitude(received, target):
-        whole = received[...].reshape(8 * NS, PL)
-        spectra = [whole[:, HB * h : HB * h + HB] for h in range(HL)]
-        for g in range(4):
-            rows = slice(2 * H * g, 2 * H * g + 2 * H)
-            out = dot(lv[0, rows, :], spectra[0])
-            for h in range(1, HL):
-                out = out + dot(lv[h, rows, :], spectra[h])
-            out = (out * lat_factor).astype(BF16)
+    def latitude(received, target, ones):
+        for h in range(HL):
+            rc[LN * h : LN * h + LN, :] = received[:, :, HB * h : HB * h + HB].reshape(LN, HB)
+        out = dot(lv[...], rc[...]) * lat_factor
+        for mm in range(2):
             for part in range(2):
-                for one in range(2):
-                    at_row = HB * (g % 2) + H * one
-                    target[g // 2, at_row : at_row + H, LN * part : LN * part + CB] = out[
-                        H * part : H * part + H, CB * one : CB * one + CB
-                    ]
+                rows = slice(2 * H * mm + H * part, 2 * H * mm + H * part + H)
+                for m in range(4):
+                    tile = tile_of(out, rows, 0, m, lane_h)
+                    if ones:
+                        tile = jnp.where(lane_h == CB, 1.0 - part, tile)
+                    target[mm, H * m : H * m + H, LN * part : LN * part + LN] = tile.astype(BF16)
 
     loads[8].wait()
 
@@ -401,38 +370,38 @@
             hid[s, i] = hidden
             post = dot(hidden, wc[1]) + vec[3:4, :]
             shape = jnp.tanh(post * (1.0 / shrink_level))
-            shrunk = (post - shrink_level * shape).astype(BF16)
+            shrunk = post - shrink_level * shape
             grad_post = (gsh[s, i].astype(F32) * (shape * shape)).astype(BF16)
             gpost[s, i] = grad_post
             grad_pre = (dot_nt(grad_post, wc[1]) * slope).astype(BF16)
             gpre[s, i] = grad_pre
-            grad_lat = dot_nt(grad_pre, wc[0]).astype(BF16)
-            for pair in range(2):
+            grad_lat = dot_nt(grad_pre, wc[0])
+            for source, target in ((shrunk, sh), (grad_lat, glat)):
                 for part in range(2):
-                    for one in range(2):
-                        rows = slice(HB * pair + H * part, HB * pair + H * part + H)
-                        lanes = slice(CB * one, CB * one + CB)
-                        from_rows = slice(HB * pair + H * one, HB * pair + H * one + H)
-                        from_lanes = slice(LN * part, LN * part + CB)
-                        sh[s, i, rows, lanes] = shrunk[from_rows, from_lanes]
-                        glat[s, i, rows, lanes] = grad_lat[from_rows, from_lanes]
+                    tiles = [
+                        source[H * m : H * m + H, LN * part : LN * part + LN] for m in range(4)
+                    ]
+                    for j, column in enumerate(dense(tiles, lane_h)):
+                        target[s, i, H * part : H * part + H, LN * j : LN * j + LN] = (
+                            column.astype(BF16)
+                        )
             return carry
 
         lax.fori_loop(0, 2, step, 0)
 
     def back(source, target):
-        spectrum = source[...].reshape(8 * H, HB)
+        out = dot(mv[...], source[...].reshape(4 * H, HB)) * lat_factor
         for h in range(HL):
-            out = dot(mv[h], spectrum) * lat_factor
-            target[:, :, HB * h : HB * h + HB] = out.reshape(NS, 8, HB).astype(BF16)
+            piece = out[LN * h : LN * h + LN, :].reshape(NS, 4, HB)
+            target[:, :, HB * h : HB * h + HB] = piece.astype(BF16)
 
     for s in range(2):
         arrived(A2 + s, recv2.at[s])
-        latitude(recv2.at[s], gsh.at[s])
+        latitude(recv2.at[s], gsh.at[s], False)
     loads[9].wait()
     for s in range(2):
         arrived(A1 + s, recv1.at[s])
-        latitude(recv1.at[s], lt.at[s])
+        latitude(recv1.at[s], lt.at[s], True)
         mix(s)
         back(glat.at[s], send4.at[s])
         spread("space", A4 + s, lambda t, s=s: send4.at[s, t], recv4.at[s])
@@ -454,11 +423,11 @@
 
     def gradient_sums(s):
         arrived(A4 + s, recv4.at[s])
-        out = dot(ev[0], recv4[s].reshape(8 * NS, PL)) * lon_factor
+        out = dot(ev[0], recv4[s].reshape(4 * NS, PL)) * lon_factor
         total = jnp.zeros((WP, LN), F32)
         for h in range(HL):
             for m in range(4):
-                grad_normed = tile_of(out, h, m)
+                grad_normed = tile_of(out, slice(0, WP), h, m, lane_w)
                 centred = cen[s, 4 * h + m]
                 product = grad_normed * centred
                 norm_sums[0] = norm_sums[0] + jnp.sum(product.reshape(WP // 8, 8, LN), axis=0)
@@ -488,10 +457,10 @@
 
     def put_mixed(s):
         arrived(A3 + s, recv3.at[s])
-        out = dot(ev[1], recv3[s].reshape(8 * NS, PL)) * lon_factor
+        out = dot(ev[1], recv3[s].reshape(4 * NS, PL)) * lon_factor
         for h in range(HL):
             for m in range(4):
-                put_members(tc, h, 4 * s + m, tile_of(out, h, m))
+                put_members(tc, h, 4 * s + m, tile_of(out, slice(0, WP), h, m, lane_w))
 
     def put_members(array, h, b, tile):
         array[h, pl.ds(b, WP, stride=8), :] = tile
@@ -569,9 +538,9 @@
     vmem = pl.BlockSpec(memory_space=pltpu.VMEM)
     stays = pl.BlockSpec(memory_space=pltpu.HBM)
     token = (HL, 1, 8, W * CB)
-    piece = (2, NS, 8, PL)
+    piece = (2, NS, 4, PL)
     spectral = (2, 2, 4 * H, 2 * LN)
-    folded = (2, 2, 4 * H, HB)
+    folded = (2, 2, 2 * H, HB)
     results = (
         jax.ShapeDtypeStruct(token, BF16),
         jax.ShapeDtypeStruct(token, BF16),
@@ -590,17 +559,18 @@
         scratch_shapes=[
             pltpu.VMEM(token, BF16),
             pltpu.VMEM(token, BF16),
-            pltpu.VMEM((2, 8 * NS, 2 * WP), BF16),
-            pltpu.VMEM((2, 2 * WP, 8 * NS), BF16),
-            pltpu.VMEM((HL, 8 * H, 8 * NS), BF16),
-            pltpu.VMEM((HL, 8 * NS, 8 * H), BF16),
+            pltpu.VMEM((2, 4 * NS, WP), BF16),
+            pltpu.VMEM((2, WP, 4 * NS), BF16),
+            pltpu.VMEM((4 * H, 4 * H), BF16),
+            pltpu.VMEM((4 * H, 4 * H), BF16),
             pltpu.VMEM((HL, 8 * WP, LN), F32),
             pltpu.VMEM((HL, 8 * WP, LN), F32),
-            pltpu.VMEM((2, 2 * WP, PL), BF16),
+            pltpu.VMEM((2, WP, PL), BF16),
             pltpu.VMEM((2, 4 * HL, WP, LN), F32),
             pltpu.VMEM((2, 4 * HL, WP, LN), F32),
         ]
         + [pltpu.VMEM(piece, BF16)] * 8
+        + [pltpu.VMEM((4 * H, HB), BF16)]
         + [pltpu.VMEM(spectral, BF16)] * 5
         + [pltpu.VMEM(folded, BF16)] * 2
         + [

time: 59.7 us -> 57.1 us (0.956)
  Pallas kernels: 58.8 us -> 56.2 us
    pallas_call x1, Pallas kernels: 57.5 us -> 54.9 us  [on_device(): pl.pallas_call(layer, out_shape=tuple((pltpu.VMEM(r.shape, r.dtype) for r...]
where the time goes in v3:
time: 57.1 us; the launch traced here: 57 us
  Pallas kernels  56.2 us (98%)
  between operations  0.8 us (1%)
    pallas_call x1, Pallas kernels, on_device(): pl.pallas_call(layer, out_shape=tuple((pltpu.VMEM(r.shape, r.dtype) for r...  54.9 us
    pallas_call x1, Pallas kernels, on_device(): pl.pallas_call(write_out, out_shape=results, in_specs=[vmem] * 8, out_spe...  1.3 us

profile of v3, /device:TPU:1, one launch (start us, length us, event | category | flops | bytes accessed | tf_op | source)
XLA Modules:
  0.0 57.0 jit_solution(17762526834743199007)
XLA Ops:
  0.6 54.9 %shard_map.179 = (bf16[3,1,8,17280]{3,2,1,0:T(8,128)(2,1)S(1)}, bf16[3,1,8,17280]{3,2,1,0:T(8,128)(2,1)S(1)}, f32[2,1,96,96]{3,2,1,0:T(8,128)S(1)}, f32[2,1,96]{...) custom-call(bf16[3,1,8,17280]{3,2,1,0:T(8,128)(2,1)} %bitcast.8, ...), custom_call_target="tpu_custom_call" | custom-call | tf_op jit(solution)/shard_map/pallas_call | solution.py:554
  55.6 1.3 %shard_map.180 = (bf16[3,1,8,17280]{3,2,1,0:T(8,128)(2,1)}, bf16[3,1,8,17280]{3,2,1,0:T(8,128)(2,1)}, f32[2,1,96,96]{3,2,1,0:T(8,128)}, f32[2,1,96]{2,1,0:T(1,12...) custom-call(bf16[3,1,8,17280]{3,2,1,0:T(8,128)(2,1)S(1)} %get-tuple-element.24.refs_0_, ...), custom_call_target="tpu_custom_call" | custom-call | tf_op jit(solution)/shard_map/pallas_call | solution.py:623

commit v4 on v3

--- a/solution.py
+++ b/solution.py
@@ -34,7 +34,7 @@
 MESH = pl.DeviceIdType.MESH
 
 RS1, AG1, A2, A1, A4, A3, RS2, AG2 = range(0, 16, 2)
-GWR, GWG, GG = range(16, 19)
+GWR, GWG = range(16, 18)
 
 
 def twiddle(length, columns):
@@ -71,11 +71,17 @@
             lat[mm, 1, :, hh, :, 0, mm] = -sin_part
             lat[mm, 1, :, hh, :, 1, mm] = cos_part
     lat = lat.reshape(4 * H, 4 * H)
+    picked = np.zeros((HL, 4, 2, LN, LN), np.float32)
+    for h in range(HL):
+        for m in range(4):
+            for q in range(2):
+                picked[h, m, q, :CB, 8 * m + 3 * q + h] = 1.0
     return (
         np.stack([lon, scaled]).astype(bf),
         np.stack([lon.T, scaled.T]).astype(bf),
         lat.astype(bf),
         lat.T.astype(bf),
+        picked.reshape(8 * HL * LN, LN).astype(bf),
     )
 
 
@@ -140,13 +146,13 @@
 
 def layer(
     x_hbm, cot_hbm, gain_hbm, shift_hbm, w1_hbm, b1_hbm, w2_hbm, b2_hbm,
-    d_hbm, e_hbm, l_hbm, m_hbm,
+    d_hbm, e_hbm, l_hbm, m_hbm, pick_hbm,
     mixed_out, gin_out, gw1_ref, gb1_ref, gw2_ref, gb2_ref, gg_ref, gs_ref,
     xv, cv, dv, ev, lv, mv, tx, tc, xn, cen, gc,
     send1, send2, send3, send4, recv1, recv2, recv3, recv4,
     rc, lt, gsh, hid, gpost, gpre, sh, glat, wc, vec,
     acc, st, rb, ags, ab, at, acc2, st2, rb2, ags2, ab2, at2,
-    gb, gr, gas, ga, ggs, ggr, small, w1_v, w2_v, b1_v, b2_v,
+    gb, gr, gas, ga, invb, terms, pick, small, w1_v, w2_v, b1_v, b2_v,
     in_sems, send_sems, recv_sems,
 ):
     me_s = lax.axis_index("space")
@@ -165,6 +171,7 @@
         pltpu.make_async_copy(b1_hbm, b1_v, in_sems.at[13]),
         pltpu.make_async_copy(w2_hbm, w2_v, in_sems.at[14]),
         pltpu.make_async_copy(b2_hbm, b2_v, in_sems.at[15]),
+        pltpu.make_async_copy(pick_hbm, pick, in_sems.at[16]),
     ]
     for load in loads:
         load.start()
@@ -186,14 +193,15 @@
     lax.fori_loop(1, NC, greet_chan, 0)
     lax.fori_loop(1, NS, greet_space, 0)
 
-    def spread(axis, index, piece, target):
+    def spread(axis, index, piece, target, slot=None):
+        slot = slot or (lambda t: target.at[t])
         count, me = (NS, me_s) if axis == "space" else (NC, me_c)
 
         def step(r, carry):
             t = lax.rem(me + r, count)
             pltpu.make_async_remote_copy(
                 src_ref=piece(t),
-                dst_ref=target.at[me],
+                dst_ref=slot(me),
                 send_sem=send_sems.at[index],
                 recv_sem=recv_sems.at[index],
                 device_id={axis: t},
@@ -202,7 +210,7 @@
             return carry
 
         lax.fori_loop(1, count, step, 0)
-        pltpu.make_async_copy(piece(me), target.at[me], recv_sems.at[index]).start()
+        pltpu.make_async_copy(piece(me), slot(me), recv_sems.at[index]).start()
 
     def arrived(index, target):
         pltpu.make_async_copy(target, target, recv_sems.at[index]).wait()
@@ -302,12 +310,11 @@
         unpack(cv, tc, h)
     loads[6].wait()
 
-    def send_cotangent(s):
+    def cotangent_spectra(s):
         for h in range(HL):
             store_dense(s, h, [members_of(tc, h, 4 * s + m) for m in range(4)])
         out = dot(dv[1], xn[s]) * lon_factor
         send2[s] = out.reshape(NS, 4, PL).astype(BF16)
-        spread("space", A2 + s, lambda t: send2.at[s, t], recv2.at[s])
 
     def share_statistics(s):
         arrived(RS1 + s, rb.at[s])
@@ -318,10 +325,12 @@
         ags[s] = jnp.where(row8 < 3, sums, jnp.where(row8 < 6, pltpu.roll(inv, 3, 0), 0.0))
         spread("chan", AG1 + s, lambda t: ags.at[s], ab.at[s])
 
-    send_cotangent(0)
+    cotangent_spectra(0)
     share_statistics(0)
     share_statistics(1)
-    send_cotangent(1)
+    spread("space", A2, lambda t: send2.at[0, t], recv2.at[0])
+    cotangent_spectra(1)
+    spread("space", A2 + 1, lambda t: send2.at[1, t], recv2.at[1])
 
     def send_normed(s):
         arrived(AG1 + s, ab.at[s, pl.ds(0, NC)])
@@ -332,7 +341,9 @@
                 column = 8 * m + h
                 mean_col = at[s, 0:WP, column : column + 1]
                 inv_col = at[s, 0:WP, column + 3 : column + 4]
-                centred = (members_of(tx, h, 4 * s + m) - mean_col) * inv_col
+                inv_tile = jnp.broadcast_to(inv_col, (WP, LN))
+                invb[s, 4 * h + m] = inv_tile
+                centred = (members_of(tx, h, 4 * s + m) - mean_col) * inv_tile
                 cen[s, 4 * h + m] = centred
                 tiles.append(centred * gain_row + shift_row)
             store_dense(s, h, tiles)
@@ -405,9 +416,8 @@
         mix(s)
         back(glat.at[s], send4.at[s])
         spread("space", A4 + s, lambda t, s=s: send4.at[s, t], recv4.at[s])
-        if s == 1:
-            spread("space", A3, lambda t: send3.at[0, t], recv3.at[0])
         back(sh.at[s], send3.at[s])
+    spread("space", A3, lambda t: send3.at[:, t], recv3, lambda t: recv3.at[:, t])
 
     for layer_at, (left, right) in enumerate(((lt, gpre), (hid, gpost))):
         outer = dot_tn(left[...].reshape(16 * H, 2 * LN), right[...].reshape(16 * H, 2 * LN))
@@ -415,16 +425,14 @@
         imag = outer[0:LN, LN:] - outer[LN:, 0:LN]
         gb[16 * layer_at : 16 * layer_at + 8] = real.reshape(8, 16, LN).astype(BF16)
         gb[16 * layer_at + 8 : 16 * layer_at + 16] = imag.reshape(8, 16, LN).astype(BF16)
-    spread("space", GWR, lambda t: gb.at[t], gr)
-    spread("space", A3 + 1, lambda t: send3.at[1, t], recv3.at[1])
 
     loads[7].wait()
+    loads[16].wait()
     norm_sums = [jnp.zeros((8, LN), F32), jnp.zeros((8, LN), F32)]
 
     def gradient_sums(s):
         arrived(A4 + s, recv4.at[s])
         out = dot(ev[0], recv4[s].reshape(4 * NS, PL)) * lon_factor
-        total = jnp.zeros((WP, LN), F32)
         for h in range(HL):
             for m in range(4):
                 grad_normed = tile_of(out, slice(0, WP), h, m, lane_w)
@@ -433,12 +441,13 @@
                 norm_sums[0] = norm_sums[0] + jnp.sum(product.reshape(WP // 8, 8, LN), axis=0)
                 norm_sums[1] = norm_sums[1] + jnp.sum(grad_normed.reshape(WP // 8, 8, LN), axis=0)
                 grad_centred = grad_normed * gain_row
-                gc[s, 4 * h + m] = grad_centred
-                one = jnp.sum(grad_centred, axis=1, keepdims=True)
-                two = jnp.sum(grad_centred * centred, axis=1, keepdims=True)
-                total = jnp.where(lane_w == 8 * m + h, one, total)
-                total = jnp.where(lane_w == 8 * m + 3 + h, two, total)
-        acc2[s, 0:WP, :] = total
+                i = 4 * h + m
+                gc[s, i] = grad_centred * invb[s, i]
+                terms[:, 2 * LN * i : 2 * LN * i + LN] = grad_centred.astype(BF16)
+                terms[:, 2 * LN * i + LN : 2 * LN * i + 2 * LN] = (
+                    grad_centred * centred
+                ).astype(BF16)
+        acc2[s, 0:WP, :] = dot(terms[...], pick[...])
         pieces_of_sums(acc2.at[s], st2.at[s])
         spread("chan", RS2 + s, lambda t: st2.at[s, t], rb2.at[s])
 
@@ -451,12 +460,18 @@
         spread("chan", AG2 + s, lambda t: ags2.at[s], ab2.at[s])
 
     share_gradient_sums(0)
-    ggs[0:1, :] = jnp.sum(norm_sums[0], axis=0, keepdims=True)
-    ggs[1:2, :] = jnp.sum(norm_sums[1], axis=0, keepdims=True)
-    spread("space", GG, lambda t: ggs, ggr)
+    row16 = lax.broadcasted_iota(jnp.int32, (16, LN), 0)
+    spare = jnp.where(
+        row16 == 1,
+        jnp.sum(norm_sums[0], axis=0, keepdims=True),
+        jnp.sum(norm_sums[1], axis=0, keepdims=True),
+    )
+    gb[CB // 16] = jnp.where(
+        (row16 == 1) | (row16 == 2), spare, gb[CB // 16].astype(F32)
+    ).astype(BF16)
+    spread("space", GWR, lambda t: gb.at[t], gr)
 
     def put_mixed(s):
-        arrived(A3 + s, recv3.at[s])
         out = dot(ev[1], recv3[s].reshape(4 * NS, PL)) * lon_factor
         for h in range(HL):
             for m in range(4):
@@ -468,20 +483,18 @@
     def put_gradient(s):
         arrived(AG2 + s, ab2.at[s, pl.ds(0, NC)])
         columns_of(ab2.at[s], at2.at[s])
+        inv = at[s]
+        lane = lax.broadcasted_iota(jnp.int32, (2 * LN, LN), 1)
+        at2[s] = at2[s] * jnp.where(lane % 8 < 3, pltpu.roll(inv, LN - 3, 1), inv)
         for h in range(HL):
             for m in range(4):
                 column = 8 * m + h
-                inv_col = at[s, 0:WP, column + 3 : column + 4]
                 first = at2[s, 0:WP, column : column + 1]
                 second = at2[s, 0:WP, column + 3 : column + 4]
                 put_members(
-                    tx,
-                    h,
-                    4 * s + m,
-                    inv_col * (gc[s, 4 * h + m] - first - cen[s, 4 * h + m] * second),
+                    tx, h, 4 * s + m, gc[s, 4 * h + m] - first - cen[s, 4 * h + m] * second
                 )
 
-    put_mixed(0)
     share_gradient_sums(1)
     put_gradient(0)
     arrived(GWR, gr)
@@ -490,14 +503,12 @@
     put_gradient(1)
     for h in range(HL):
         pack(tx, gin_out, h)
+    arrived(A3, recv3)
+    put_mixed(0)
     put_mixed(1)
     for h in range(HL):
         pack(tc, mixed_out, h)
 
-    arrived(GG, ggr)
-    both = jnp.sum(ggr[...], axis=0)
-    gg_ref[...] = both[0:1, 0:CB]
-    gs_ref[...] = both[1:2, 0:CB]
     arrived(GWG, ga)
     for layer_at, (gw_ref, gbias_ref) in enumerate(((gw1_ref, gb1_ref), (gw2_ref, gb2_ref))):
         for part in range(2):
@@ -505,6 +516,9 @@
             block = ga[at_piece : at_piece + 8].astype(F32).reshape(LN, LN)
             gw_ref[part, 0] = block[0:CB, 0:CB]
             gbias_ref[part] = block[CB : CB + 1, 0:CB]
+            if layer_at == 0 and part == 0:
+                gg_ref[...] = block[CB + 1 : CB + 2, 0:CB]
+                gs_ref[...] = block[CB + 2 : CB + 3, 0:CB]
 
     for s in range(2):
         sent(RS1 + s, rb.at[s], NC)
@@ -514,10 +528,10 @@
         sent(A2 + s, recv2.at[s], NS)
         sent(A1 + s, recv1.at[s], NS)
         sent(A4 + s, recv4.at[s], NS)
-        sent(A3 + s, recv3.at[s], NS)
+    half = recv3.at[:, pl.ds(0, NS - 1)]
+    pltpu.make_async_copy(half, half, send_sems.at[A3]).wait()
     sent(GWR, gr, NS)
     sent(GWG, ga, NS)
-    sent(GG, ggr, NS)
 
 
 def write_out(*refs):
@@ -533,7 +547,7 @@
 
 
 def on_device(members, gain, shift, w_first, b_first, w_second, b_second, cotangent):
-    lon_out, lon_back, lat_out, lat_back = (jnp.asarray(t) for t in tables())
+    lon_out, lon_back, lat_out, lat_back, picks = (jnp.asarray(t) for t in tables())
     anywhere = pl.BlockSpec(memory_space=pl.ANY)
     vmem = pl.BlockSpec(memory_space=pltpu.VMEM)
     stays = pl.BlockSpec(memory_space=pltpu.HBM)
@@ -554,7 +568,7 @@
     outs = pl.pallas_call(
         layer,
         out_shape=tuple(pltpu.VMEM(r.shape, r.dtype) for r in results),
-        in_specs=[stays] * 12,
+        in_specs=[stays] * 13,
         out_specs=tuple([vmem] * 8),
         scratch_shapes=[
             pltpu.VMEM(token, BF16),
@@ -591,16 +605,17 @@
             pltpu.VMEM((NS, 16, LN), BF16),
             pltpu.VMEM((16, LN), BF16),
             pltpu.VMEM((NS, 16, LN), BF16),
-            pltpu.VMEM((2, LN), F32),
-            pltpu.VMEM((NS, 2, LN), F32),
+            pltpu.VMEM((2, 4 * HL, WP, LN), F32),
+            pltpu.VMEM((WP, 8 * HL * LN), BF16),
+            pltpu.VMEM((8 * HL * LN, LN), BF16),
             pltpu.VMEM((2, 1, CB), F32),
             pltpu.VMEM((2, 1, CB, CB), BF16),
             pltpu.VMEM((2, 1, CB, CB), BF16),
             pltpu.VMEM((2, 1, CB), F32),
             pltpu.VMEM((2, 1, CB), F32),
-            pltpu.SemaphoreType.DMA((16,)),
-            pltpu.SemaphoreType.DMA((19,)),
-            pltpu.SemaphoreType.DMA((19,)),
+            pltpu.SemaphoreType.DMA((17,)),
+            pltpu.SemaphoreType.DMA((18,)),
+            pltpu.SemaphoreType.DMA((18,)),
         ],
         compiler_params=pltpu.CompilerParams(
             collective_id=0, has_side_effects=True, vmem_limit_bytes=60 * 1024 * 1024
@@ -618,6 +633,7 @@
         lon_back,
         lat_out,
         lat_back,
+        picks,
     )
     outs = [pltpu.with_memory_space_constraint(o, pltpu.VMEM) for o in outs]
     mixed, grad_input, gw1, gb1, gw2, gb2, gg, gs = pl.pallas_call(

time: 57.1 us -> 59.9 us (1.049)
  Pallas kernels: 56.2 us -> 59 us
    pallas_call x1, Pallas kernels: 54.9 us -> 57.7 us  [on_device(): pl.pallas_call(layer, out_shape=tuple((pltpu.VMEM(r.shape, r.dtype) for r...]
where the time goes in v4:
time: 59.9 us; the launch traced here: 59.8 us
  Pallas kernels  59 us (98%)
  between operations  0.8 us (1%)
    pallas_call x1, Pallas kernels, on_device(): pl.pallas_call(layer, out_shape=tuple((pltpu.VMEM(r.shape, r.dtype) for r...  57.7 us
    pallas_call x1, Pallas kernels, on_device(): pl.pallas_call(write_out, out_shape=results, in_specs=[vmem] * 8, out_spe...  1.3 us

profile of v4, /device:TPU:1, one launch (start us, length us, event | category | flops | bytes accessed | tf_op | source)
XLA Modules:
  0.0 59.8 jit_solution(1899770885541879010)
XLA Ops:
  0.6 57.7 %shard_map.188 = (bf16[3,1,8,17280]{3,2,1,0:T(8,128)(2,1)S(1)}, bf16[3,1,8,17280]{3,2,1,0:T(8,128)(2,1)S(1)}, f32[2,1,96,96]{3,2,1,0:T(8,128)S(1)}, f32[2,1,96]{...) custom-call(bf16[3,1,8,17280]{3,2,1,0:T(8,128)(2,1)} %bitcast.8, ...), custom_call_target="tpu_custom_call" | custom-call | tf_op jit(solution)/shard_map/pallas_call | solution.py:568
  58.4 1.3 %shard_map.189 = (bf16[3,1,8,17280]{3,2,1,0:T(8,128)(2,1)}, bf16[3,1,8,17280]{3,2,1,0:T(8,128)(2,1)}, f32[2,1,96,96]{3,2,1,0:T(8,128)}, f32[2,1,96]{2,1,0:T(1,12...) custom-call(bf16[3,1,8,17280]{3,2,1,0:T(8,128)(2,1)S(1)} %get-tuple-element.24.refs_0_, ...), custom_call_target="tpu_custom_call" | custom-call | tf_op jit(solution)/shard_map/pallas_call | solution.py:639

commit v5 on v4

--- a/solution.py
+++ b/solution.py
@@ -326,11 +326,11 @@
         spread("chan", AG1 + s, lambda t: ags.at[s], ab.at[s])
 
     cotangent_spectra(0)
+    spread("space", A2, lambda t: send2.at[0, t], recv2.at[0])
     share_statistics(0)
-    share_statistics(1)
-    spread("space", A2, lambda t: send2.at[0, t], recv2.at[0])
     cotangent_spectra(1)
     spread("space", A2 + 1, lambda t: send2.at[1, t], recv2.at[1])
+    share_statistics(1)
 
     def send_normed(s):
         arrived(AG1 + s, ab.at[s, pl.ds(0, NC)])
@@ -416,8 +416,9 @@
         mix(s)
         back(glat.at[s], send4.at[s])
         spread("space", A4 + s, lambda t, s=s: send4.at[s, t], recv4.at[s])
+        if s == 1:
+            spread("space", A3, lambda t: send3.at[0, t], recv3.at[0])
         back(sh.at[s], send3.at[s])
-    spread("space", A3, lambda t: send3.at[:, t], recv3, lambda t: recv3.at[:, t])
 
     for layer_at, (left, right) in enumerate(((lt, gpre), (hid, gpost))):
         outer = dot_tn(left[...].reshape(16 * H, 2 * LN), right[...].reshape(16 * H, 2 * LN))
@@ -425,6 +426,9 @@
         imag = outer[0:LN, LN:] - outer[LN:, 0:LN]
         gb[16 * layer_at : 16 * layer_at + 8] = real.reshape(8, 16, LN).astype(BF16)
         gb[16 * layer_at + 8 : 16 * layer_at + 16] = imag.reshape(8, 16, LN).astype(BF16)
+
+    spread("space", GWR, lambda t: gb.at[t], gr)
+    spread("space", A3 + 1, lambda t: send3.at[1, t], recv3.at[1])
 
     loads[7].wait()
     loads[16].wait()
@@ -460,17 +464,6 @@
         spread("chan", AG2 + s, lambda t: ags2.at[s], ab2.at[s])
 
     share_gradient_sums(0)
-    row16 = lax.broadcasted_iota(jnp.int32, (16, LN), 0)
-    spare = jnp.where(
-        row16 == 1,
-        jnp.sum(norm_sums[0], axis=0, keepdims=True),
-        jnp.sum(norm_sums[1], axis=0, keepdims=True),
-    )
-    gb[CB // 16] = jnp.where(
-        (row16 == 1) | (row16 == 2), spare, gb[CB // 16].astype(F32)
-    ).astype(BF16)
-    spread("space", GWR, lambda t: gb.at[t], gr)
-
     def put_mixed(s):
         out = dot(ev[1], recv3[s].reshape(4 * NS, PL)) * lon_factor
         for h in range(HL):
@@ -495,30 +488,37 @@
                     tx, h, 4 * s + m, gc[s, 4 * h + m] - first - cen[s, 4 * h + m] * second
                 )
 
+    arrived(A3, recv3.at[0])
+    put_mixed(0)
     share_gradient_sums(1)
     put_gradient(0)
     arrived(GWR, gr)
-    gas[...] = jnp.sum(gr[...].astype(F32), axis=0).astype(BF16)
+    gas[0:16] = jnp.sum(gr[...].astype(F32), axis=0).astype(BF16)
+    row8 = lax.broadcasted_iota(jnp.int32, (8, LN), 0)
+    gas[16:24] = jnp.where(
+        row8 == 0,
+        jnp.sum(norm_sums[0], axis=0, keepdims=True),
+        jnp.where(row8 == 1, jnp.sum(norm_sums[1], axis=0, keepdims=True), 0.0),
+    ).astype(BF16)
     spread("space", GWG, lambda t: gas, ga)
     put_gradient(1)
     for h in range(HL):
         pack(tx, gin_out, h)
-    arrived(A3, recv3)
-    put_mixed(0)
+    arrived(A3 + 1, recv3.at[1])
     put_mixed(1)
     for h in range(HL):
         pack(tc, mixed_out, h)
 
     arrived(GWG, ga)
+    both = jnp.sum(ga[:, 16:24].astype(F32), axis=0)
+    gg_ref[...] = both[0:1, 0:CB]
+    gs_ref[...] = both[1:2, 0:CB]
     for layer_at, (gw_ref, gbias_ref) in enumerate(((gw1_ref, gb1_ref), (gw2_ref, gb2_ref))):
         for part in range(2):
             at_piece = 16 * layer_at + 8 * part
-            block = ga[at_piece : at_piece + 8].astype(F32).reshape(LN, LN)
+            block = ga[at_piece : at_piece + 8, 0:16].astype(F32).reshape(LN, LN)
             gw_ref[part, 0] = block[0:CB, 0:CB]
             gbias_ref[part] = block[CB : CB + 1, 0:CB]
-            if layer_at == 0 and part == 0:
-                gg_ref[...] = block[CB + 1 : CB + 2, 0:CB]
-                gs_ref[...] = block[CB + 2 : CB + 3, 0:CB]
 
     for s in range(2):
         sent(RS1 + s, rb.at[s], NC)
@@ -528,8 +528,8 @@
         sent(A2 + s, recv2.at[s], NS)
         sent(A1 + s, recv1.at[s], NS)
         sent(A4 + s, recv4.at[s], NS)
-    half = recv3.at[:, pl.ds(0, NS - 1)]
-    pltpu.make_async_copy(half, half, send_sems.at[A3]).wait()
+    sent(A3, recv3.at[0], NS)
+    sent(A3 + 1, recv3.at[1], NS)
     sent(GWR, gr, NS)
     sent(GWG, ga, NS)
 
@@ -603,8 +603,8 @@
         + [
             pltpu.VMEM((NS, 16, LN), BF16),
             pltpu.VMEM((NS, 16, LN), BF16),
-            pltpu.VMEM((16, LN), BF16),
-            pltpu.VMEM((NS, 16, LN), BF16),
+            pltpu.VMEM((24, LN), BF16),
+            pltpu.VMEM((NS, 24, LN), BF16),
             pltpu.VMEM((2, 4 * HL, WP, LN), F32),
             pltpu.VMEM((WP, 8 * HL * LN), BF16),
             pltpu.VMEM((8 * HL * LN, LN), BF16),

time: 59.9 us -> 56.1 us (0.937)
  Pallas kernels: 59 us -> 55.2 us
    pallas_call x1, Pallas kernels: 57.7 us -> 53.9 us  [on_device(): pl.pallas_call(layer, out_shape=tuple((pltpu.VMEM(r.shape, r.dtype) for r...]
where the time goes in v5:
time: 56.1 us; the launch traced here: 56 us
  Pallas kernels  55.2 us (98%)
  between operations  0.8 us (1%)
    pallas_call x1, Pallas kernels, on_device(): pl.pallas_call(layer, out_shape=tuple((pltpu.VMEM(r.shape, r.dtype) for r...  53.9 us
    pallas_call x1, Pallas kernels, on_device(): pl.pallas_call(write_out, out_shape=results, in_specs=[vmem] * 8, out_spe...  1.3 us

profile of v5, /device:TPU:1, one launch (start us, length us, event | category | flops | bytes accessed | tf_op | source)
XLA Modules:
  0.0 56.0 jit_solution(16187342459315778919)
XLA Ops:
  0.6 53.9 %shard_map.188 = (bf16[3,1,8,17280]{3,2,1,0:T(8,128)(2,1)S(1)}, bf16[3,1,8,17280]{3,2,1,0:T(8,128)(2,1)S(1)}, f32[2,1,96,96]{3,2,1,0:T(8,128)S(1)}, f32[2,1,96]{...) custom-call(bf16[3,1,8,17280]{3,2,1,0:T(8,128)(2,1)} %bitcast.8, ...), custom_call_target="tpu_custom_call" | custom-call | tf_op jit(solution)/shard_map/pallas_call | solution.py:568
  54.5 1.3 %shard_map.189 = (bf16[3,1,8,17280]{3,2,1,0:T(8,128)(2,1)}, bf16[3,1,8,17280]{3,2,1,0:T(8,128)(2,1)}, f32[2,1,96,96]{3,2,1,0:T(8,128)}, f32[2,1,96]{2,1,0:T(1,12...) custom-call(bf16[3,1,8,17280]{3,2,1,0:T(8,128)(2,1)S(1)} %get-tuple-element.24.refs_0_, ...), custom_call_target="tpu_custom_call" | custom-call | tf_op jit(solution)/shard_map/pallas_call | solution.py:639

commit v6 on v5

--- a/solution.py
+++ b/solution.py
@@ -416,9 +416,9 @@
         mix(s)
         back(glat.at[s], send4.at[s])
         spread("space", A4 + s, lambda t, s=s: send4.at[s, t], recv4.at[s])
-        if s == 1:
-            spread("space", A3, lambda t: send3.at[0, t], recv3.at[0])
-        back(sh.at[s], send3.at[s])
+    back(sh.at[0], send3.at[0])
+    spread("space", A3, lambda t: send3.at[0, t], recv3.at[0])
+    back(sh.at[1], send3.at[1])
 
     for layer_at, (left, right) in enumerate(((lt, gpre), (hid, gpost))):
         outer = dot_tn(left[...].reshape(16 * H, 2 * LN), right[...].reshape(16 * H, 2 * LN))

time: 56.1 us -> 56 us (level)
  no operation moved by 1% of the time
where the time goes in v6:
time: 56 us
  Pallas kernels  55.2 us (99%)
  between operations  0.8 us (1%)
    pallas_call x1, Pallas kernels, on_device(): pl.pallas_call(layer, out_shape=tuple((pltpu.VMEM(r.shape, r.dtype) for r...  53.9 us
    pallas_call x1, Pallas kernels, on_device(): pl.pallas_call(write_out, out_shape=results, in_specs=[vmem] * 8, out_spe...  1.3 us

profile of v6, /device:TPU:1, one launch (start us, length us, event | category | flops | bytes accessed | tf_op | source)
XLA Modules:
  0.0 56.0 jit_solution(9195277776551552097)
XLA Ops:
  0.6 53.9 %shard_map.188 = (bf16[3,1,8,17280]{3,2,1,0:T(8,128)(2,1)S(1)}, bf16[3,1,8,17280]{3,2,1,0:T(8,128)(2,1)S(1)}, f32[2,1,96,96]{3,2,1,0:T(8,128)S(1)}, f32[2,1,96]{...) custom-call(bf16[3,1,8,17280]{3,2,1,0:T(8,128)(2,1)} %bitcast.8, ...), custom_call_target="tpu_custom_call" | custom-call | tf_op jit(solution)/shard_map/pallas_call | solution.py:568
  54.5 1.3 %shard_map.189 = (bf16[3,1,8,17280]{3,2,1,0:T(8,128)(2,1)}, bf16[3,1,8,17280]{3,2,1,0:T(8,128)(2,1)}, f32[2,1,96,96]{3,2,1,0:T(8,128)}, f32[2,1,96]{2,1,0:T(1,12...) custom-call(bf16[3,1,8,17280]{3,2,1,0:T(8,128)(2,1)S(1)} %get-tuple-element.24.refs_0_, ...), custom_call_target="tpu_custom_call" | custom-call | tf_op jit(solution)/shard_map/pallas_call | solution.py:639
